TPU v7x, 128 devices: a whole 4x4x4 slice. The times are simulated.
128 devices in a mesh: mgroup: 16 (over y_hi, z, core), msub: 8 (over x, y_lo).
Axes of the slice: x: 4, y: 4 (y_hi: 2, y_lo: 2; y = y_hi * 2 + y_lo), z: 4, core: 2. Of those that a mesh axis runs over, the one named last changes fastest.
Arguments:
- in_modes: int32 [128, 2], P(('mgroup', 'msub')), may hold values from 0 to 31
- back_first: bfloat16 [128, 1024, 2048], P(('mgroup', 'msub')), may hold values from -192 to 192
- back_second: bfloat16 [128, 1024, 2048], P(('mgroup', 'msub')), may hold values from -512 to 512
Outputs:
- mask_first: float32 [1024, 2048], P(('mgroup', 'msub'))
- mask_second: float32 [1024, 2048], P(('mgroup', 'msub'))
Inputs may be any that keep to these rules, and one draw needn't show every extreme that they name: `in_modes`: each row holds a mode's row order and column order.
All inputs are finite; a program needn't handle non-finite values.
Results may differ from a plain program's by a relative error of at most 0.013.
Values may be sent and summed in bfloat16 or wider, within the bound.
No kernel may reach another device: no remote copies, remote signals or barrier semaphores. Data moves between devices by JAX's collectives and lax.ppermute only.
A program may use at most 128 MiB of HBM per device.

v0:
```python
import functools
import math

import jax
import jax.numpy as jnp
import numpy as np
from jax import lax
from jax.experimental import pallas as pl
from jax.experimental.pallas import tpu as pltpu
from jax.sharding import Mesh
from jax.sharding import PartitionSpec as P

ORDERS = 32
SPAN = 24.0
AXES = ("yh", "z", "core", "x", "yl")
BF16 = jnp.bfloat16
F32 = jnp.float32
ANY = pl.BlockSpec(memory_space=pl.ANY)
VMEM = pl.BlockSpec(memory_space=pltpu.VMEM)
SMEM = pl.BlockSpec(memory_space=pltpu.SMEM)
DMA = pltpu.SemaphoreType.DMA


def params(mib):
    return pltpu.CompilerParams(vmem_limit_bytes=mib << 20)


def hermite_table(cells):
    index = np.arange(cells, dtype=np.float32)
    points = ((index - np.float32(cells / 2) + np.float32(0.5)) * np.float32(SPAN / cells)).astype(np.float32)
    before = np.zeros_like(points)
    current = (np.float32(math.pi ** (-0.25)) * np.exp(np.float32(-0.5) * points * points)).astype(np.float32)
    collected = []
    for order in range(ORDERS):
        collected.append(current)
        following = (
            np.float32(math.sqrt(2.0 / (order + 1))) * points * current
            - np.float32(math.sqrt(order / (order + 1.0))) * before
        ).astype(np.float32)
        before, current = (current, following)
    return np.stack(collected, axis=0)


def chirp_halves(cells):
    half = cells // 2
    index = np.arange(half, dtype=np.int64)
    offset = index[:, None] - index[None, :]
    square = offset * offset % (2 * cells)
    phase = square.astype(np.float64) * (math.pi / cells)
    factor = cells ** (-0.5)
    real = (np.cos(phase) * factor).astype(np.float32)
    imag = (np.sin(phase) * factor).astype(np.float32)
    even = offset % 2 == 0
    out = []
    for keep in (even, ~even):
        r = np.where(keep, real, 0.0)
        i = np.where(keep, imag, 0.0)
        out.append((r.astype(jnp.bfloat16), i.astype(jnp.bfloat16)))
    return out


def soften(intersection):
    half = intersection.shape[-1] // 2
    real_part = intersection[..., :half]
    imag_part = intersection[..., half:]
    denom = jnp.sqrt(real_part * real_part + imag_part * imag_part + 1.0)
    return intersection / jnp.concatenate([denom, denom], axis=-1)


def swap_cores(block):
    return lax.ppermute(block, "core", [(0, 1), (1, 0)])


def row_of(modes, columns, core):
    picked = columns[:, :, core].reshape(512, ORDERS)
    lanes = lax.broadcasted_iota(jnp.int32, picked.shape, 1)
    return jnp.sum(jnp.where(lanes == modes[0, 0], picked, 0.0), axis=1, keepdims=True)


def bits_of(spot):
    return (spot & 1) ^ (spot >> 1), spot >> 1


def owner_codes():
    out = []
    for yh in range(2):
        for z in range(4):
            for x in range(4):
                for yl in range(2):
                    (ax, bx), (ay, by), (az, bz) = bits_of(x), bits_of(yh * 2 + yl), bits_of(z)
                    out.append((ax * 4 + ay * 2 + az, bx * 4 + by * 2 + bz))
    return out


CODES = owner_codes()


def place_of(block, core):
    a, b = CODES[block]
    return a * 8 + b + core * (7 * b - 7 * a)


def device_groups():
    def device(a, b, core):
        x, y, z = ((a >> k & 1) ^ (3 * (b >> k & 1)) for k in (2, 1, 0))
        return ((((y >> 1) * 4 + z) * 2 + core) * 4 + x) * 2 + (y & 1)

    over_a = [[[device(a, b, core) for a in range(8)] for b in range(8)] for core in range(2)]
    over_b = [[[device(a, b, core) for b in range(8)] for a in range(8)] for core in range(2)]
    return over_a[0] + over_b[1], over_b[0] + over_a[1]


WIDE, NARROW = device_groups()


def first_kernel(away, modes, table, columns, *refs):
    if away:
        back, out, buf, sems = refs
        got = None
    else:
        got, back, out, buf, sems = refs
    core = lax.axis_index("core")
    if away:
        core = 1 - core
    copies = [
        pltpu.make_async_copy(back.at[k // 4, k % 4, core], buf.at[k], sems.at[k]) for k in range(8)
    ]
    for copy in copies:
        copy.start()
    row_func = row_of(modes, columns, core)
    col_func = table[pl.ds(modes[0, 1], 1), :]
    cells = col_func.shape[1]
    for k in range(8):
        copies[k].wait()
        for j in range(8):
            block = k * 8 + j
            place = place_of(block, core)
            field = (row_func[block * 8 : block * 8 + 8] * col_func).astype(BF16).astype(F32)
            for plane in range(2):
                span = slice(plane * cells, (plane + 1) * cells)
                value = buf[k, j * 8 : j * 8 + 8, span].astype(F32) * field
                if not away:
                    value = value + got[place, :, span].astype(F32)
                out[place, :, span] = value.astype(BF16)


def first_product(modes, table, columns, back, got=None):
    width = back.shape[-1]
    away = got is None
    return pl.pallas_call(
        functools.partial(first_kernel, away),
        out_shape=jax.ShapeDtypeStruct((64, 8, width), BF16),
        in_specs=[SMEM, VMEM, VMEM] + ([] if away else [VMEM]) + [ANY],
        out_specs=VMEM,
        scratch_shapes=[pltpu.VMEM((8, 64, width), BF16), DMA((8,))],
        compiler_params=params(14),
        name="first_away" if away else "first_keep",
    )(modes, table, columns, *(() if away else (got,)), back)


def spread_half(modes, table, columns, mask, even, odd, plus, minus, sums, diffs, core, slot):
    row_func = row_of(modes, columns, core)
    col_func = table[pl.ds(modes[0, 1], 1), :]
    cells = col_func.shape[1]
    half = cells // 2
    for pair in range(32):
        kept = []
        for block in (2 * pair, 2 * pair + 1):
            place = place_of(block, core)
            field = (row_func[block * 8 : block * 8 + 8] * col_func).astype(BF16).astype(F32)
            kept.append((mask[place, :, :cells].astype(F32) * field, mask[place, :, cells:].astype(F32) * (-field)))
        rows = slice(pair * 16, pair * 16 + 16)
        for plane in range(2):
            both = jnp.concatenate([kept[0][plane], kept[1][plane]], axis=0)
            span = slice(plane * half, (plane + 1) * half)
            plus[rows, span] = (both[:, :half] + both[:, half:]).astype(BF16)
            minus[rows, span] = (both[:, :half] - both[:, half:]).astype(BF16)
    for n in range(4):
        span = slice(n * 256, (n + 1) * 256)
        e = jnp.dot(plus[...], even[:, :, :, :, span].reshape(cells, 256), preferred_element_type=F32)
        o = jnp.dot(minus[...], odd[:, :, :, :, span].reshape(cells, 256), preferred_element_type=F32)
        plane, at = n // 2, (n % 2) * 256
        for shift, value in ((0, e + o), (half, e - o)):
            value = (-value if plane else value).astype(BF16)
            top, bottom = value[:256], value[256:]
            where = slice(at + shift, at + shift + 256)
            sums[plane, :, slot, :, where] = (top + bottom).reshape(4, 64, 256)
            diffs[plane, :, slot, :, where] = (top - bottom).reshape(4, 64, 256)


def second_half(even, odd, sums, diffs, back, out, core):
    cells = sums.shape[-1]
    rows_even = even[:, :, core].reshape(512, cells)
    rows_odd = odd[:, :, core].reshape(512, cells)
    for n in range(4):
        span = slice(n * 256, (n + 1) * 256)
        e = jnp.dot(rows_even, sums[:, :, :, :, span].reshape(cells, 256), preferred_element_type=F32)
        o = jnp.dot(rows_odd, diffs[:, :, :, :, span].reshape(cells, 256), preferred_element_type=F32)
        other = slice(cells + n * 256, cells + (n + 1) * 256)
        for h, value in ((0, e + o), (1, e - o)):
            real, imag = value[:256], value[256:]
            back_real = back[h, :, :, span].reshape(256, 256).astype(F32)
            back_imag = back[h, :, :, other].reshape(256, 256).astype(F32)
            new_real = back_real * real + back_imag * imag
            new_imag = back_imag * real - back_real * imag
            for j in range(32):
                place = place_of(h * 32 + j, core)
                out[place, :, span] = new_real[j * 8 : j * 8 + 8].astype(BF16)
                out[place, :, other] = new_imag[j * 8 : j * 8 + 8].astype(BF16)


def spread_kernel(modes, table, columns, mask, even, odd, sums, diffs, plus, minus):
    core = lax.axis_index("core")
    spread_half(modes, table, columns, mask, even, odd, plus, minus, sums, diffs, core, 0)


def spread_own(modes, table, columns, mask, even, odd):
    cells = even.shape[-1]
    shape = jax.ShapeDtypeStruct((2, 4, 1, 64, cells), BF16)
    return pl.pallas_call(
        spread_kernel,
        out_shape=(shape, shape),
        in_specs=[SMEM] + [VMEM] * 5,
        out_specs=(VMEM, VMEM),
        scratch_shapes=[pltpu.VMEM((512, cells), BF16)] * 2,
        compiler_params=params(20),
        name="spread_own",
    )(modes, table, columns, mask, even, odd)


def arrive_kernel(
    modes, table, columns, mask, even, odd, own_sums, own_diffs, back, out, sums, diffs, buf, plus, minus, sem
):
    core = lax.axis_index("core")
    other = 1 - core
    copy = pltpu.make_async_copy(back.at[:, :, other], buf, sem)
    copy.start()
    spread_half(modes, table, columns, mask, even, odd, plus, minus, sums, diffs, other, other)
    sums[:, :, core] = own_sums[:, :, 0]
    diffs[:, :, core] = own_diffs[:, :, 0]
    copy.wait()
    second_half(even, odd, sums, diffs, buf, out, other)


def arrive_away(modes, table, columns, mask, even, odd, own_sums, own_diffs, back):
    width = back.shape[-1]
    cells = width // 2
    shape = jax.ShapeDtypeStruct((2, 4, 2, 64, cells), BF16)
    return pl.pallas_call(
        arrive_kernel,
        out_shape=(jax.ShapeDtypeStruct((64, 8, width), BF16), shape, shape),
        in_specs=[SMEM] + [VMEM] * 7 + [ANY],
        out_specs=(VMEM, VMEM, VMEM),
        scratch_shapes=[pltpu.VMEM((2, 4, 64, width), BF16)] + [pltpu.VMEM((512, cells), BF16)] * 2 + [DMA],
        compiler_params=params(28),
        name="arrive_away",
    )(modes, table, columns, mask, even, odd, own_sums, own_diffs, back)


def keep_kernel(even, odd, sums, diffs, back, out, buf, sem):
    core = lax.axis_index("core")
    copy = pltpu.make_async_copy(back.at[:, :, core], buf, sem)
    copy.start()
    copy.wait()
    second_half(even, odd, sums, diffs, buf, out, core)


def arrive_keep(even, odd, sums, diffs, back):
    width = back.shape[-1]
    return pl.pallas_call(
        keep_kernel,
        out_shape=jax.ShapeDtypeStruct((64, 8, width), BF16),
        in_specs=[VMEM] * 4 + [ANY],
        out_specs=VMEM,
        scratch_shapes=[pltpu.VMEM((2, 4, 64, width), BF16), DMA],
        compiler_params=params(20),
        name="arrive_keep",
    )(even, odd, sums, diffs, back)


def exchange(blocks, groups):
    return lax.all_to_all(blocks, AXES, 0, 0, tiled=True, axis_index_groups=groups)


def total(parts):
    kept = [parts[k].astype(F32) for k in range(parts.shape[0])]
    while len(kept) > 1:
        kept = [kept[k] + kept[k + 1] for k in range(0, len(kept), 2)]
    return kept[0]


def scatter_rows(both):
    width = both.shape[-1]
    wide = exchange(both.reshape(8, 64, width), WIDE)
    partial = total(wide).astype(BF16)
    parts = exchange(partial.reshape(8, 8, width), NARROW)
    return total(parts)


def gather_rows(own):
    rows, width = own.shape
    near = exchange(jnp.broadcast_to(own[None], (8, rows, width)), NARROW)
    near = near.reshape(1, 8 * rows, width)
    wide = exchange(jnp.broadcast_to(near, (8, 8 * rows, width)), WIDE)
    return wide.reshape(64, rows, width)


def body(modes, back_first, back_second):
    cells = back_first.shape[1]
    scale_all = float(128) ** (-0.5)
    host_table = hermite_table(cells)
    table = jnp.asarray(host_table)
    columns = jnp.asarray(host_table.T.copy()).reshape(2, 4, 2, 64, ORDERS)
    (even_r, even_i), (odd_r, odd_i) = jax.tree.map(jnp.asarray, chirp_halves(cells))
    even = jnp.block([[even_r, -even_i], [even_i, even_r]]).reshape(2, 4, 2, 64, cells)
    odd = jnp.block([[odd_r, -odd_i], [odd_i, odd_r]]).reshape(2, 4, 2, 64, cells)
    back_first = back_first.reshape(2, 4, 2, 64, 2 * cells)
    back_second = back_second.reshape(2, 4, 2, 64, 2 * cells)
    got = swap_cores(first_product(modes, table, columns, back_first))
    summed = scatter_rows(first_product(modes, table, columns, back_first, got))
    mask_first = soften(summed * scale_all)
    mine = gather_rows(mask_first.astype(BF16))
    other = swap_cores(mine)
    own = spread_own(modes, table, columns, mine, even, odd)
    away, sums, diffs = arrive_away(modes, table, columns, other, even, odd, *own, back_second)
    got = swap_cores(away)
    keep = arrive_keep(even, odd, sums, diffs, back_second)
    summed = scatter_rows((keep.astype(F32) + got.astype(F32)).astype(BF16))
    mask_second = soften(summed * scale_all)
    return (mask_first, mask_second)


def solution(mesh):
    fine = Mesh(mesh.devices.reshape(2, 4, 2, 4, 2), AXES)
    placed = (P(AXES, None), P(AXES, None, None), P(AXES, None, None))
    return jax.shard_map(
        body, mesh=fine, in_specs=placed, out_specs=(P(AXES, None), P(AXES, None)), check_vma=False
    )
```

profile of v0, /device:TPU:0, one launch (start us, length us, event | category | flops | bytes accessed | tf_op | source)
XLA Modules:
  0.0 136.7 jit_solution(6693436247503155215)
XLA Ops:
  0.6 2.2 %copy-done.3 = bf16[1,1024,2048]{2,1,0:T(8,128)(2,1)S(1)} copy-done((bf16[1,1024,2048]{2,1,0:T(8,128)(2,1)S(1)}, bf16[1,1024,2048]{2,1,0:T(8,128)(2,1)}, u32[]{:S(2)}) %copy-start.3) | copy-done | bytes 4194328
  2.8 1.0 copy-done.4
  3.9 0.9 copy-done.6
  4.8 0.7 copy-done.8
  5.4 1.5 %first_away.1 = bf16[64,8,2048]{2,1,0:T(8,128)(2,1)S(1)} custom-call(s32[1,2]{1,0:T(1,128)S(1)} %copy-done.8, f32[32,1024]{1,0:T(8,128)S(1)} %copy-done.6, f32[2,4,2,64,32]{4,3,2,1,0:T(8,128)S(1)} %copy-done.4, bf16[2,4,2,64,2048]{4,3,2,1,0:T(8,128)(2,1)S(1)} %bitcast.23), custom_call_target="tpu_custom_call" | custom-call | tf_op jit(solution)/shard_map/first_away/pallas_call | solution.py:150
  7.0 4.1 %collective-permute-done.refs_0_ = bf16[64,8,2048]{2,1,0:T(8,128)(2,1)S(1)} collective-permute-done((bf16[64,8,2048]{2,1,0:T(8,128)(2,1)S(1)}, bf16[64,8,2048]{2,1,0:T(8,128)(2,1)S(1)}, u32[]{:S(2)}, u32[]{:S(2)}) %collective-permute-start) | collective-permute-done | bytes 2097184 | tf_op jit(solution)/shard_map/ppermute | solution.py:71
  11.2 1.8 %first_keep.1 = bf16[64,8,2048]{2,1,0:T(8,128)(2,1)S(1)} custom-call(s32[1,2]{1,0:T(1,128)S(1)} %copy-done.8, f32[32,1024]{1,0:T(8,128)S(1)} %copy-done.6, f32[2,4,2,64,32]{4,3,2,1,0:T(8,128)S(1)} %copy-done.4, bf16[64,8,2048]{2,1,0:T(8,128)(2,1)S(1)} %collective-permute-done.refs_0_, bf16[2,4,2,64,2048]{4,3,2,1,0:T(8,128)(2,1)S(1)} %bitcast.24), custom_call_target="tpu_custom_call" | custom-call | tf_op jit(solution)/shard_map/first_keep/pallas_call | solution.py:150
  13.0 21.5 %all_to_all.30 = bf16[8,64,2048]{2,1,0:T(8,128)(2,1)S(1)} all-to-all(bf16[8,64,2048]{2,1,0:T(8,128)(2,1)S(1)} %bitcast.25), channel_id=1, replica_groups={{0,16,1,17,2,18,3,19},{48,32,49,33,50,34,51,35},{65,81,64,80,67,83,66,8..., dimensions={0} | all-to-all | bytes 4194304 | tf_op jit(solution)/shard_map/all_to_all | solution.py:282
  34.8 17.5 %all_to_all.31 = bf16[8,8,2048]{2,1,0:T(8,128)(2,1)S(1)} all-to-all(bf16[8,8,2048]{2,1,0:T(8,128)(2,1)S(1)} %fusion), channel_id=1, replica_groups={{0,48,65,113,6,54,71,119},{16,32,81,97,22,38,87,103},{1,49,64,112,7,55,..., dimensions={0} | all-to-all | bytes 524288 | tf_op jit(solution)/shard_map/all_to_all | solution.py:282
  52.5 12.7 %all_to_all.32 = bf16[8,8,2048]{2,1,0:T(8,128)(2,1)S(1)} all-to-all(bf16[8,8,2048]{2,1,0:T(8,128)(2,1)S(1)} %broadcast_in_dim.16), channel_id=1, replica_groups={{0,48,65,113,6,54,71,119},{16,32,81,97,22,38,87,103},{1,49,64,112,7,55,..., dimensions={0} | all-to-all | bytes 524288 | tf_op jit(solution)/shard_map/all_to_all | solution.py:282
  65.5 19.2 %all_to_all.33 = bf16[8,64,2048]{2,1,0:T(8,128)(2,1)S(1)} all-to-all(bf16[8,64,2048]{2,1,0:T(8,128)(2,1)S(1)} %broadcast_in_dim.18), channel_id=1, replica_groups={{0,16,1,17,2,18,3,19},{48,32,49,33,50,34,51,35},{65,81,64,80,67,83,66,8..., dimensions={0} | all-to-all | bytes 4194304 | tf_op jit(solution)/shard_map/all_to_all | solution.py:282
  84.7 3.3 %spread_own.1 = (bf16[2,4,1,64,1024]{4,3,2,1,0:T(8,128)(2,1)S(1)}, bf16[2,4,1,64,1024]{4,3,2,1,0:T(8,128)(2,1)S(1)}) custom-call(s32[1,2]{1,0:T(1,128)S(1)} %copy-done.9, f32[32,1024]{1,0:T(8,128)S(1)} %copy-done.7, f32[2,4,2,64,32]{4,3,2,1,0:T(8,128)S(1)} %copy-done.5, bf16[64,8,2048]{2,1,0:T(8,128)(2,1)S(1)} %bitcast.27, ...), custom_call_target="tpu_custom_call" | custom-call | tf_op jit(solution)/shard_map/spread_own/pallas_call | solution.py:220
  88.0 0.8 collective-permute-done.1.mask
  88.8 6.5 %arrive_away.1 = (bf16[64,8,2048]{2,1,0:T(8,128)(2,1)S(1)}, bf16[2,4,2,64,1024]{4,3,2,1,0:T(8,128)(2,1)S(1)}, bf16[2,4,2,64,1024]{4,3,2,1,0:T(8,128)(2,1)S(1)}) custom-call(s32[1,2]{1,0:T(1,128)S(1)} %copy-done.9, f32[32,1024]{1,0:T(8,128)S(1)} %copy-done.7, f32[2,4,2,64,32]{4,3,2,1,0:T(8,128)S(1)} %copy-done.5, ...), custom_call_target="tpu_custom_call" | custom-call | tf_op jit(solution)/shard_map/arrive_away/pallas_call | solution.py:249
  95.7 3.1 %arrive_keep.1 = bf16[64,8,2048]{2,1,0:T(8,128)(2,1)S(1)} custom-call(bf16[2,4,2,64,1024]{4,3,2,1,0:T(8,128)(2,1)S(1)} %copy-done.1, bf16[2,4,2,64,1024]{4,3,2,1,0:T(8,128)(2,1)S(1)} %copy-done, bf16[2,4,2,64,1024]{4,3,2,1,0:T(8,128)(2,1)S(1)} %get-tuple-element.9.sums, bf16[2,4,2,64,1024]{4,3,2,1,0:T(8,128)(2,1)S(1)} %get-tuple-element.10.diffs, ...), custom_call_target="tpu_custom_call" | custom-call | tf_op jit(solution)/shard_map/arrive_keep/pallas_call | solution.py:270
  98.8 0.9 collective-permute-done.2
  99.7 2.1 %add_convert_fusion = bf16[64,8,2048]{2,1,0:T(8,128)(2,1)} fusion(bf16[64,8,2048]{2,1,0:T(8,128)(2,1)S(1)} %collective-permute-done.2, bf16[64,8,2048]{2,1,0:T(8,128)(2,1)S(1)} %arrive_keep.1), kind=kLoop, calls=%fused_computation | loop fusion | flops 4194304 | bytes 6291456 | tf_op jit(solution)/shard_map/convert_element_type | solution.py:328
  101.9 3.6 %all-to-all-start.4 = ((bf16[8,64,2048]{2,1,0:T(8,128)(2,1)}), bf16[8,64,2048]{2,1,0:T(8,128)(2,1)S(1)}, u32[]{:S(2)}, u32[]{:S(2)}) async-start(bf16[8,64,2048]{2,1,0:T(8,128)(2,1)} %bitcast.9), calls=%async_computation.4 | async-start | bytes 4194304 | tf_op jit(solution)/shard_map/all_to_all | solution.py:282
  105.5 15.8 %all-to-all-done.4 = bf16[8,64,2048]{2,1,0:T(8,128)(2,1)S(1)} async-done(((bf16[8,64,2048]{2,1,0:T(8,128)(2,1)}), bf16[8,64,2048]{2,1,0:T(8,128)(2,1)S(1)}, u32[]{:S(2)}, u32[]{:S(2)}) %all-to-all-start.4) | async-done | bytes 2097184 | tf_op jit(solution)/shard_map/all_to_all | solution.py:282
  121.3 1.0 fusion.1
  122.3 3.4 %all-to-all-start.5 = ((bf16[8,8,2048]{2,1,0:T(8,128)(2,1)}), bf16[8,8,2048]{2,1,0:T(8,128)(2,1)S(1)}, u32[]{:S(2)}, u32[]{:S(2)}) async-start(bf16[8,8,2048]{2,1,0:T(8,128)(2,1)} %fusion.1), calls=%async_computation.5 | async-start | bytes 524288 | tf_op jit(solution)/shard_map/all_to_all | solution.py:282
  125.8 0.7 maximum_divide_fusion
  126.4 9.5 %all-to-all-done.5 = bf16[8,8,2048]{2,1,0:T(8,128)(2,1)S(1)} async-done(((bf16[8,8,2048]{2,1,0:T(8,128)(2,1)}), bf16[8,8,2048]{2,1,0:T(8,128)(2,1)S(1)}, u32[]{:S(2)}, u32[]{:S(2)}) %all-to-all-start.5) | async-done | bytes 262176 | tf_op jit(solution)/shard_map/all_to_all | solution.py:282
  136.0 0.7 maximum_divide_fusion.2
  (28 shorter events, 1.3 us)
Async XLA Ops:
  0.6 2.2 %copy-start.3 = (bf16[1,1024,2048]{2,1,0:T(8,128)(2,1)S(1)}, bf16[1,1024,2048]{2,1,0:T(8,128)(2,1)}, u32[]{:S(2)}) copy-start(bf16[1,1024,2048]{2,1,0:T(8,128)(2,1)} %param.10) | copy-start | bytes 12582916
  2.8 1.0 copy-start.4
  3.9 0.9 copy-start.6
  4.8 0.7 copy-start.8
  6.9 4.2 %collective-permute-start = (bf16[64,8,2048]{2,1,0:T(8,128)(2,1)S(1)}, bf16[64,8,2048]{2,1,0:T(8,128)(2,1)S(1)}, u32[]{:S(2)}, u32[]{:S(2)}) collective-permute-start(bf16[64,8,2048]{2,1,0:T(8,128)(2,1)S(1)} %first_away.1), channel_id=1, source_target_pairs={{0,8},{8,0},{1,9},{9,1},{2,10},{10,2},{3,11},{11,3},{4,12},{12,4},... | collective-permute-start | bytes 6291464 | tf_op jit(solution)/shard_map/ppermute | solution.py:71
  65.2 19.5 %copy-start.5 = (f32[2,4,2,64,32]{4,3,2,1,0:T(8,128)S(1)}, f32[2,4,2,64,32]{4,3,2,1,0:T(8,128)}, u32[]{:S(2)}) copy-start(f32[2,4,2,64,32]{4,3,2,1,0:T(8,128)} %constant.25.columns) | copy-start | bytes 393220
  65.2 19.5 %copy-start.7 = (f32[32,1024]{1,0:T(8,128)S(1)}, f32[32,1024]{1,0:T(8,128)}, u32[]{:S(2)}) copy-start(f32[32,1024]{1,0:T(8,128)} %constant.16.clone.table) | copy-start | bytes 393220
  65.4 19.2 %copy-start = (bf16[2,4,2,64,1024]{4,3,2,1,0:T(8,128)(2,1)S(1)}, bf16[2,4,2,64,1024]{4,3,2,1,0:T(8,128)(2,1)}, u32[]{:S(2)}) copy-start(bf16[2,4,2,64,1024]{4,3,2,1,0:T(8,128)(2,1)} %constant.35.odd) | copy-start | bytes 6291460
  65.4 19.2 %copy-start.1 = (bf16[2,4,2,64,1024]{4,3,2,1,0:T(8,128)(2,1)S(1)}, bf16[2,4,2,64,1024]{4,3,2,1,0:T(8,128)(2,1)}, u32[]{:S(2)}) copy-start(bf16[2,4,2,64,1024]{4,3,2,1,0:T(8,128)(2,1)} %constant.30.even) | copy-start | bytes 6291460
  65.4 19.2 %copy-start.9 = (s32[1,2]{1,0:T(1,128)S(1)}, s32[1,2]{1,0:T(1,128)}, u32[]{:S(2)}) copy-start(s32[1,2]{1,0:T(1,128)} %modes.7) | copy-start | bytes 28
  84.6 4.2 %copy-start.2 = (bf16[1,1024,2048]{2,1,0:T(8,128)(2,1)S(1)}, bf16[1,1024,2048]{2,1,0:T(8,128)(2,1)}, u32[]{:S(2)}) copy-start(bf16[1,1024,2048]{2,1,0:T(8,128)(2,1)} %param.11) | copy-start | bytes 12582916
  84.6 4.2 %collective-permute-start.1 = (bf16[64,8,2048]{2,1,0:T(8,128)(2,1)S(1)}, bf16[64,8,2048]{2,1,0:T(8,128)(2,1)S(1)}, u32[]{:S(2)}, u32[]{:S(2)}) collective-permute-start(bf16[64,8,2048]{2,1,0:T(8,128)(2,1)S(1)} %bitcast.26), channel_id=1, source_target_pairs={{0,8},{8,0},{1,9},{9,1},{2,10},{10,2},{3,11},{11,3},{4,12},{12,4},... | collective-permute-start | bytes 6291464 | tf_op jit(solution)/shard_map/ppermute | solution.py:71
  95.3 4.4 %collective-permute-start.2 = (bf16[64,8,2048]{2,1,0:T(8,128)(2,1)S(1)}, bf16[64,8,2048]{2,1,0:T(8,128)(2,1)S(1)}, u32[]{:S(2)}, u32[]{:S(2)}) collective-permute-start(bf16[64,8,2048]{2,1,0:T(8,128)(2,1)S(1)} %get-tuple-element.11), channel_id=1, source_target_pairs={{0,8},{8,0},{1,9},{9,1},{2,10},{10,2},{3,11},{11,3},{4,12},{12,4},... | collective-permute-start | bytes 6291464 | tf_op jit(solution)/shard_map/ppermute | solution.py:71
  101.9 19.4 %all-to-all-start.4 = ((bf16[8,64,2048]{2,1,0:T(8,128)(2,1)}), bf16[8,64,2048]{2,1,0:T(8,128)(2,1)S(1)}, u32[]{:S(2)}, u32[]{:S(2)}) async-start(bf16[8,64,2048]{2,1,0:T(8,128)(2,1)} %bitcast.9), calls=%async_computation.4 | async-start | bytes 4194304 | tf_op jit(solution)/shard_map/all_to_all | solution.py:282
  122.3 13.6 %all-to-all-start.5 = ((bf16[8,8,2048]{2,1,0:T(8,128)(2,1)}), bf16[8,8,2048]{2,1,0:T(8,128)(2,1)S(1)}, u32[]{:S(2)}, u32[]{:S(2)}) async-start(bf16[8,8,2048]{2,1,0:T(8,128)(2,1)} %fusion.1), calls=%async_computation.5 | async-start | bytes 524288 | tf_op jit(solution)/shard_map/all_to_all | solution.py:282
where the time goes:
time: 137 us
  blocking collectives  70.9 us (52%)
  waiting for transfers between devices  31.2 us (23%)
  Pallas kernels  16.2 us (12%)
  starting transfers between devices  7.5 us (5%)
  local copies, waits for them, and re-layouts  5.07 us (4%)
  other arithmetic  5.03 us (4%)
    all_to_all x4, blocking collectives, exchange(): lax.all_to_all(blocks, AXES, 0, 0, tiled=True, axis_index_groups=groups)  70.9 us
    all_to_all x2, waiting for transfers between devices, exchange(): lax.all_to_all(blocks, AXES, 0, 0, tiled=True, axis_index_groups=groups)  25.3 us
    all_to_all x2, starting transfers between devices, exchange(): lax.all_to_all(blocks, AXES, 0, 0, tiled=True, axis_index_groups=groups)  7.01 us
    pallas_call x1, Pallas kernels, arrive_away(): pl.pallas_call(arrive_kernel, out_shape=(jax.ShapeDtypeStruct((64, 8, wid...  6.52 us
    ppermute x3, waiting for transfers between devices, swap_cores(): return lax.ppermute(block, 'core', [(0, 1), (1, 0)])  5.88 us
    unnamed x20, local copies, waits for them, and re-layouts  4.81 us
    pallas_call x1, Pallas kernels, spread_own(): pl.pallas_call(spread_kernel, out_shape=(shape, shape), in_specs=[SMEM] +...  3.31 us
    pallas_call x2, Pallas kernels, first_product(): pl.pallas_call(functools.partial(first_kernel, away), out_shape=jax.Shape...  3.3 us
  transfers between devices with their start and end apart: 5, of which 5 were waited for; matrix products, arithmetic and copies ran while one was open for 1% of the time, Pallas kernels for 5%

commit v1 on v0

--- a/solution.py
+++ b/solution.py
@@ -113,12 +113,7 @@
 WIDE, NARROW = device_groups()
 
 
-def first_kernel(away, modes, table, columns, *refs):
-    if away:
-        back, out, buf, sems = refs
-        got = None
-    else:
-        got, back, out, buf, sems = refs
+def first_kernel(away, modes, table, columns, back, out, buf, sems):
     core = lax.axis_index("core")
     if away:
         core = 1 - core
@@ -138,24 +133,21 @@
             field = (row_func[block * 8 : block * 8 + 8] * col_func).astype(BF16).astype(F32)
             for plane in range(2):
                 span = slice(plane * cells, (plane + 1) * cells)
-                value = buf[k, j * 8 : j * 8 + 8, span].astype(F32) * field
-                if not away:
-                    value = value + got[place, :, span].astype(F32)
-                out[place, :, span] = value.astype(BF16)
-
-
-def first_product(modes, table, columns, back, got=None):
+                out[place, :, span] = (buf[k, j * 8 : j * 8 + 8, span].astype(F32) * field).astype(BF16)
+
+
+def first_product(modes, table, columns, back, away):
     width = back.shape[-1]
-    away = got is None
     return pl.pallas_call(
         functools.partial(first_kernel, away),
         out_shape=jax.ShapeDtypeStruct((64, 8, width), BF16),
-        in_specs=[SMEM, VMEM, VMEM] + ([] if away else [VMEM]) + [ANY],
+        in_specs=[SMEM, VMEM, VMEM, ANY],
         out_specs=VMEM,
         scratch_shapes=[pltpu.VMEM((8, 64, width), BF16), DMA((8,))],
-        compiler_params=params(14),
+        compiler_params=params(60 if away else 14),
+        cost_estimate=pl.CostEstimate(flops=2 << 20, bytes_accessed=4 << 20, transcendentals=0),
         name="first_away" if away else "first_keep",
-    )(modes, table, columns, *(() if away else (got,)), back)
+    )(modes, table, columns, back)
 
 
 def spread_half(modes, table, columns, mask, even, odd, plus, minus, sums, diffs, core, slot):
@@ -283,26 +275,51 @@
 
 
 def total(parts):
-    kept = [parts[k].astype(F32) for k in range(parts.shape[0])]
+    kept = [parts[k].astype(F32) for k in range(len(parts))]
     while len(kept) > 1:
         kept = [kept[k] + kept[k + 1] for k in range(0, len(kept), 2)]
     return kept[0]
 
 
-def scatter_rows(both):
+def halve_rows(both):
     width = both.shape[-1]
-    wide = exchange(both.reshape(8, 64, width), WIDE)
-    partial = total(wide).astype(BF16)
-    parts = exchange(partial.reshape(8, 8, width), NARROW)
-    return total(parts)
-
-
-def gather_rows(own):
-    rows, width = own.shape
-    near = exchange(jnp.broadcast_to(own[None], (8, rows, width)), NARROW)
-    near = near.reshape(1, 8 * rows, width)
-    wide = exchange(jnp.broadcast_to(near, (8, 8 * rows, width)), WIDE)
-    return wide.reshape(64, rows, width)
+    return total(exchange(both.reshape(8, 64, width), WIDE)).astype(BF16)
+
+
+def own_place():
+    pairs = [bits_of(lax.axis_index("x")), bits_of(lax.axis_index("yh") * 2 + lax.axis_index("yl"))]
+    pairs.append(bits_of(lax.axis_index("z")))
+    a, b = (pairs[0][k] * 4 + pairs[1][k] * 2 + pairs[2][k] for k in range(2))
+    return b + lax.axis_index("core") * (a - b)
+
+
+def mask_kernel(scale, near, low, own, every):
+    cells = near.shape[-1] // 2
+    for block in range(8):
+        rows = slice(block * 8, block * 8 + 8)
+        real = total([near[k, rows, :cells] for k in range(8)]) * scale
+        imag = total([near[k, rows, cells:] for k in range(8)]) * scale
+        size = jnp.sqrt(real * real + imag * imag + 1.0)
+        for span, part in ((slice(0, cells), real), (slice(cells, 2 * cells), imag)):
+            part = part / size
+            every[block, :, span] = part
+            part = part.astype(BF16)
+            for k in range(8):
+                low[k, rows, span] = part
+    own[...] = every[own_place()]
+
+
+def mask_rows(near, scale):
+    width = near.shape[-1]
+    return pl.pallas_call(
+        functools.partial(mask_kernel, scale),
+        out_shape=(jax.ShapeDtypeStruct((8, 64, width), BF16), jax.ShapeDtypeStruct((8, width), F32)),
+        in_specs=[VMEM],
+        out_specs=(VMEM, VMEM),
+        scratch_shapes=[pltpu.VMEM((8, 8, width), F32)],
+        compiler_params=params(12),
+        name="mask_rows",
+    )(near)
 
 
 def body(modes, back_first, back_second):
@@ -316,17 +333,21 @@
     odd = jnp.block([[odd_r, -odd_i], [odd_i, odd_r]]).reshape(2, 4, 2, 64, cells)
     back_first = back_first.reshape(2, 4, 2, 64, 2 * cells)
     back_second = back_second.reshape(2, 4, 2, 64, 2 * cells)
-    got = swap_cores(first_product(modes, table, columns, back_first))
-    summed = scatter_rows(first_product(modes, table, columns, back_first, got))
-    mask_first = soften(summed * scale_all)
-    mine = gather_rows(mask_first.astype(BF16))
+    got = swap_cores(first_product(modes, table, columns, back_first, True))
+    keep = first_product(modes, table, columns, back_first, False)
+    partial = halve_rows((keep.astype(F32) + got.astype(F32)).astype(BF16))
+    width = 2 * cells
+    near = exchange(jnp.broadcast_to(partial[None], (8, 64, width)), NARROW)
+    low, mask_first = mask_rows(near, scale_all)
+    mine = exchange(low, WIDE).reshape(64, 8, width)
     other = swap_cores(mine)
     own = spread_own(modes, table, columns, mine, even, odd)
     away, sums, diffs = arrive_away(modes, table, columns, other, even, odd, *own, back_second)
     got = swap_cores(away)
     keep = arrive_keep(even, odd, sums, diffs, back_second)
-    summed = scatter_rows((keep.astype(F32) + got.astype(F32)).astype(BF16))
-    mask_second = soften(summed * scale_all)
+    partial = halve_rows((keep.astype(F32) + got.astype(F32)).astype(BF16))
+    parts = exchange(partial.reshape(8, 8, width), NARROW)
+    mask_second = soften(total(parts) * scale_all)
     return (mask_first, mask_second)
 
 

time: 137 us -> 129 us (0.942)
  waiting for transfers between devices: 31.2 us -> 2.01 us
  blocking collectives: 70.9 us -> 99.6 us
  starting transfers between devices: 7.5 us -> 1.01 us
  Pallas kernels: 16.2 us -> 19.6 us
  local copies, waits for them, and re-layouts: 5.07 us -> 2.45 us
  other arithmetic: 5.03 us -> 3.06 us
    all_to_all x4 -> x5, blocking collectives: 70.9 us -> 99.6 us  [exchange(): lax.all_to_all(blocks, AXES, 0, 0, tiled=True, axis_index_groups=groups)]
    all_to_all x2 -> x0, waiting for transfers between devices: 25.3 us -> none  [exchange(): lax.all_to_all(blocks, AXES, 0, 0, tiled=True, axis_index_groups=groups)]
    all_to_all x2 -> x0, starting transfers between devices: 7.01 us -> none  [exchange(): lax.all_to_all(blocks, AXES, 0, 0, tiled=True, axis_index_groups=groups)]
    ppermute x3, waiting for transfers between devices: 5.88 us -> 2.01 us  [swap_cores(): return lax.ppermute(block, 'core', [(0, 1), (1, 0)])]
    unnamed x20 -> x14, local copies, waits for them, and re-layouts: 4.81 us -> 2.21 us
    pallas_call x2, Pallas kernels: 3.3 us -> 5.65 us  [first_product(): pl.pallas_call(functools.partial(first_kernel, away), out_shape=jax.Shape...]
  transfers between devices with their start and end apart: 5 -> 3, of which waited for: 5 -> 3; matrix products, arithmetic and copies ran while one was open for 1% -> 0% of each run, Pallas kernels for 5% -> 6%
where the time goes in v1:
time: 129 us; the launch traced here: 128 us
  blocking collectives  99.6 us (77%)
  Pallas kernels  19.6 us (15%)
  other arithmetic  3.06 us (2%)
  local copies, waits for them, and re-layouts  2.45 us (2%)
  waiting for transfers between devices  2.01 us (2%)
    all_to_all x5, blocking collectives, exchange(): lax.all_to_all(blocks, AXES, 0, 0, tiled=True, axis_index_groups=groups)  99.6 us
    pallas_call x1, Pallas kernels, arrive_away(): pl.pallas_call(arrive_kernel, out_shape=(jax.ShapeDtypeStruct((64, 8, wid...  6.36 us
    pallas_call x2, Pallas kernels, first_product(): pl.pallas_call(functools.partial(first_kernel, away), out_shape=jax.Shape...  5.65 us
    pallas_call x1, Pallas kernels, spread_own(): pl.pallas_call(spread_kernel, out_shape=(shape, shape), in_specs=[SMEM] +...  3.24 us
    pallas_call x1, Pallas kernels, arrive_keep(): pl.pallas_call(keep_kernel, out_shape=jax.ShapeDtypeStruct((64, 8, width)...  3.02 us
  transfers between devices with their start and end apart: 3, of which 3 were waited for; matrix products, arithmetic and copies ran while one was open for 0% of the time, Pallas kernels for 6%

profile of v1, /device:TPU:0, one launch (start us, length us, event | category | flops | bytes accessed | tf_op | source)
XLA Modules:
  0.0 128.4 jit_solution(12533165047565064058)
XLA Ops:
  0.7 4.2 %first_away.1 = bf16[64,8,2048]{2,1,0:T(8,128)(2,1)} custom-call(s32[1,2]{1,0:T(1,128)} %modes.7, f32[32,1024]{1,0:T(8,128)} %constant.16.clone.table, f32[2,4,2,64,32]{4,3,2,1,0:T(8,128)} %constant.25.columns, bf16[2,4,2,64,2048]{4,3,2,1,0:T(8,128)(2,1)} %bitcast.15), custom_call_target="tpu_custom_call" | custom-call | flops 2097152 | bytes 4194304 | tf_op jit(solution)/shard_map/first_away/pallas_call | solution.py:141
  4.8 0.1 collective-permute-start
  5.0 2.2 %copy-done.3 = bf16[1,1024,2048]{2,1,0:T(8,128)(2,1)S(1)} copy-done((bf16[1,1024,2048]{2,1,0:T(8,128)(2,1)S(1)}, bf16[1,1024,2048]{2,1,0:T(8,128)(2,1)}, u32[]{:S(2)}) %copy-start.3) | copy-done | bytes 4194328
  7.1 1.5 %first_keep.1 = bf16[64,8,2048]{2,1,0:T(8,128)(2,1)S(1)} custom-call(s32[1,2]{1,0:T(1,128)S(1)} %copy-done.6, f32[32,1024]{1,0:T(8,128)S(1)} %copy-done.5, f32[2,4,2,64,32]{4,3,2,1,0:T(8,128)S(1)} %copy-done.4, bf16[2,4,2,64,2048]{4,3,2,1,0:T(8,128)(2,1)S(1)} %bitcast.16), custom_call_target="tpu_custom_call" | custom-call | flops 2097152 | bytes 4194304 | tf_op jit(solution)/shard_map/first_keep/pallas_call | solution.py:141
  8.6 0.6 collective-permute-done
  9.3 0.9 add_convert_fusion.1
  10.2 21.5 %all_to_all.25 = bf16[8,64,2048]{2,1,0:T(8,128)(2,1)S(1)} all-to-all(bf16[8,64,2048]{2,1,0:T(8,128)(2,1)S(1)} %bitcast.19), channel_id=1, replica_groups={{0,16,1,17,2,18,3,19},{48,32,49,33,50,34,51,35},{65,81,64,80,67,83,66,8..., dimensions={0} | all-to-all | bytes 4194304 | tf_op jit(solution)/shard_map/all_to_all | solution.py:274
  31.7 0.3 fusion
  32.0 0.2 broadcast_in_dim.9
  32.3 27.4 %all_to_all.26.near = bf16[8,64,2048]{2,1,0:T(8,128)(2,1)S(1)} all-to-all(bf16[8,64,2048]{2,1,0:T(8,128)(2,1)S(1)} %broadcast_in_dim.9), channel_id=1, replica_groups={{0,48,65,113,6,54,71,119},{16,32,81,97,22,38,87,103},{1,49,64,112,7,55,..., dimensions={0} | all-to-all | bytes 4194304 | tf_op jit(solution)/shard_map/all_to_all | solution.py:274
  59.6 1.3 mask_rows.1
  60.9 19.1 %all_to_all.27 = bf16[8,64,2048]{2,1,0:T(8,128)(2,1)S(1)} all-to-all(bf16[8,64,2048]{2,1,0:T(8,128)(2,1)S(1)} %get-tuple-element.10), channel_id=1, replica_groups={{0,16,1,17,2,18,3,19},{48,32,49,33,50,34,51,35},{65,81,64,80,67,83,66,8..., dimensions={0} | all-to-all | bytes 4194304 | tf_op jit(solution)/shard_map/all_to_all | solution.py:274
  80.1 0.3 collective-permute-start.1
  80.4 3.2 %spread_own.1 = (bf16[2,4,1,64,1024]{4,3,2,1,0:T(8,128)(2,1)S(1)}, bf16[2,4,1,64,1024]{4,3,2,1,0:T(8,128)(2,1)S(1)}) custom-call(s32[1,2]{1,0:T(1,128)S(1)} %copy-done.6, f32[32,1024]{1,0:T(8,128)S(1)} %copy-done.5, f32[2,4,2,64,32]{4,3,2,1,0:T(8,128)S(1)} %copy-done.4, bf16[64,8,2048]{2,1,0:T(8,128)(2,1)S(1)} %bitcast.18, ...), custom_call_target="tpu_custom_call" | custom-call | tf_op jit(solution)/shard_map/spread_own/pallas_call | solution.py:212
  83.7 0.6 collective-permute-done.1.mask
  84.2 6.4 %arrive_away.1 = (bf16[64,8,2048]{2,1,0:T(8,128)(2,1)S(1)}, bf16[2,4,2,64,1024]{4,3,2,1,0:T(8,128)(2,1)S(1)}, bf16[2,4,2,64,1024]{4,3,2,1,0:T(8,128)(2,1)S(1)}) custom-call(s32[1,2]{1,0:T(1,128)S(1)} %copy-done.6, f32[32,1024]{1,0:T(8,128)S(1)} %copy-done.5, f32[2,4,2,64,32]{4,3,2,1,0:T(8,128)S(1)} %copy-done.4, ...), custom_call_target="tpu_custom_call" | custom-call | tf_op jit(solution)/shard_map/arrive_away/pallas_call | solution.py:241
  90.6 0.6 collective-permute-start.2
  91.2 3.0 %arrive_keep.1 = bf16[64,8,2048]{2,1,0:T(8,128)(2,1)S(1)} custom-call(bf16[2,4,2,64,1024]{4,3,2,1,0:T(8,128)(2,1)S(1)} %copy-done.1, bf16[2,4,2,64,1024]{4,3,2,1,0:T(8,128)(2,1)S(1)} %copy-done, bf16[2,4,2,64,1024]{4,3,2,1,0:T(8,128)(2,1)S(1)} %get-tuple-element.13.sums, bf16[2,4,2,64,1024]{4,3,2,1,0:T(8,128)(2,1)S(1)} %get-tuple-element.14.diffs, ...), custom_call_target="tpu_custom_call" | custom-call | tf_op jit(solution)/shard_map/arrive_keep/pallas_call | solution.py:262
  94.2 0.8 collective-permute-done.2
  95.0 0.8 add_convert_fusion
  95.8 18.9 %all_to_all.28 = bf16[8,64,2048]{2,1,0:T(8,128)(2,1)S(1)} all-to-all(bf16[8,64,2048]{2,1,0:T(8,128)(2,1)S(1)} %bitcast.20), channel_id=1, replica_groups={{0,16,1,17,2,18,3,19},{48,32,49,33,50,34,51,35},{65,81,64,80,67,83,66,8..., dimensions={0} | all-to-all | bytes 4194304 | tf_op jit(solution)/shard_map/all_to_all | solution.py:274
  114.7 0.3 fusion.1
  115.0 12.7 %all_to_all.29 = bf16[8,8,2048]{2,1,0:T(8,128)(2,1)S(1)} all-to-all(bf16[8,8,2048]{2,1,0:T(8,128)(2,1)S(1)} %fusion.1), channel_id=1, replica_groups={{0,48,65,113,6,54,71,119},{16,32,81,97,22,38,87,103},{1,49,64,112,7,55,..., dimensions={0} | all-to-all | bytes 524288 | tf_op jit(solution)/shard_map/all_to_all | solution.py:274
  127.8 0.7 maximum_divide_fusion
  (15 shorter events, 0.1 us)
Async XLA Ops:
  0.6 4.3 %copy-start.4 = (f32[2,4,2,64,32]{4,3,2,1,0:T(8,128)S(1)}, f32[2,4,2,64,32]{4,3,2,1,0:T(8,128)}, u32[]{:S(2)}) copy-start(f32[2,4,2,64,32]{4,3,2,1,0:T(8,128)} %constant.25.columns) | copy-start | bytes 393220
  0.6 4.3 %copy-start.5 = (f32[32,1024]{1,0:T(8,128)S(1)}, f32[32,1024]{1,0:T(8,128)}, u32[]{:S(2)}) copy-start(f32[32,1024]{1,0:T(8,128)} %constant.16.clone.table) | copy-start | bytes 393220
  0.7 4.3 %copy-start.6 = (s32[1,2]{1,0:T(1,128)S(1)}, s32[1,2]{1,0:T(1,128)}, u32[]{:S(2)}) copy-start(s32[1,2]{1,0:T(1,128)} %modes.7) | copy-start | bytes 28
  4.8 4.5 %collective-permute-start = (bf16[64,8,2048]{2,1,0:T(8,128)(2,1)}, bf16[64,8,2048]{2,1,0:T(8,128)(2,1)S(1)}, u32[]{:S(2)}, u32[]{:S(2)}) collective-permute-start(bf16[64,8,2048]{2,1,0:T(8,128)(2,1)} %first_away.1), channel_id=1, source_target_pairs={{0,8},{8,0},{1,9},{9,1},{2,10},{10,2},{3,11},{11,3},{4,12},{12,4},... | collective-permute-start | bytes 6291464 | tf_op jit(solution)/shard_map/ppermute | solution.py:71
  5.0 2.2 %copy-start.3 = (bf16[1,1024,2048]{2,1,0:T(8,128)(2,1)S(1)}, bf16[1,1024,2048]{2,1,0:T(8,128)(2,1)}, u32[]{:S(2)}) copy-start(bf16[1,1024,2048]{2,1,0:T(8,128)(2,1)} %param.10) | copy-start | bytes 12582916
  60.9 19.5 %copy-start = (bf16[2,4,2,64,1024]{4,3,2,1,0:T(8,128)(2,1)S(1)}, bf16[2,4,2,64,1024]{4,3,2,1,0:T(8,128)(2,1)}, u32[]{:S(2)}) copy-start(bf16[2,4,2,64,1024]{4,3,2,1,0:T(8,128)(2,1)} %constant.35.odd) | copy-start | bytes 6291460
  60.9 19.5 %copy-start.1 = (bf16[2,4,2,64,1024]{4,3,2,1,0:T(8,128)(2,1)S(1)}, bf16[2,4,2,64,1024]{4,3,2,1,0:T(8,128)(2,1)}, u32[]{:S(2)}) copy-start(bf16[2,4,2,64,1024]{4,3,2,1,0:T(8,128)(2,1)} %constant.30.even) | copy-start | bytes 6291460
  80.1 4.2 %copy-start.2 = (bf16[1,1024,2048]{2,1,0:T(8,128)(2,1)S(1)}, bf16[1,1024,2048]{2,1,0:T(8,128)(2,1)}, u32[]{:S(2)}) copy-start(bf16[1,1024,2048]{2,1,0:T(8,128)(2,1)} %param.11) | copy-start | bytes 12582916
  80.1 4.2 %collective-permute-start.1 = (bf16[64,8,2048]{2,1,0:T(8,128)(2,1)S(1)}, bf16[64,8,2048]{2,1,0:T(8,128)(2,1)S(1)}, u32[]{:S(2)}, u32[]{:S(2)}) collective-permute-start(bf16[64,8,2048]{2,1,0:T(8,128)(2,1)S(1)} %bitcast.17), channel_id=1, source_target_pairs={{0,8},{8,0},{1,9},{9,1},{2,10},{10,2},{3,11},{11,3},{4,12},{12,4},... | collective-permute-start | bytes 6291464 | tf_op jit(solution)/shard_map/ppermute | solution.py:71
  90.6 4.4 %collective-permute-start.2 = (bf16[64,8,2048]{2,1,0:T(8,128)(2,1)S(1)}, bf16[64,8,2048]{2,1,0:T(8,128)(2,1)S(1)}, u32[]{:S(2)}, u32[]{:S(2)}) collective-permute-start(bf16[64,8,2048]{2,1,0:T(8,128)(2,1)S(1)} %get-tuple-element.15), channel_id=1, source_target_pairs={{0,8},{8,0},{1,9},{9,1},{2,10},{10,2},{3,11},{11,3},{4,12},{12,4},... | collective-permute-start | bytes 6291464 | tf_op jit(solution)/shard_map/ppermute | solution.py:71

commit v2 on v1

--- a/solution.py
+++ b/solution.py
@@ -113,27 +113,38 @@
 WIDE, NARROW = device_groups()
 
 
-def first_kernel(away, modes, table, columns, back, out, buf, sems):
+def first_kernel(away, modes, table_in, columns_in, back, out, table, columns, buf, ready, loads, sems, stores):
     core = lax.axis_index("core")
     if away:
         core = 1 - core
+    heads = [
+        pltpu.make_async_copy(table_in, table, loads.at[0]),
+        pltpu.make_async_copy(columns_in.at[:, :, core], columns.at[:, :, 0], loads.at[1]),
+    ]
     copies = [
         pltpu.make_async_copy(back.at[k // 4, k % 4, core], buf.at[k], sems.at[k]) for k in range(8)
     ]
-    for copy in copies:
+    for copy in heads + copies:
         copy.start()
-    row_func = row_of(modes, columns, core)
+    for copy in heads:
+        copy.wait()
+    row_func = row_of(modes, columns, 0)
     col_func = table[pl.ds(modes[0, 1], 1), :]
     cells = col_func.shape[1]
+    sent = []
     for k in range(8):
         copies[k].wait()
         for j in range(8):
             block = k * 8 + j
-            place = place_of(block, core)
             field = (row_func[block * 8 : block * 8 + 8] * col_func).astype(BF16).astype(F32)
             for plane in range(2):
                 span = slice(plane * cells, (plane + 1) * cells)
-                out[place, :, span] = (buf[k, j * 8 : j * 8 + 8, span].astype(F32) * field).astype(BF16)
+                ready[block, :, span] = (buf[k, j * 8 : j * 8 + 8, span].astype(F32) * field).astype(BF16)
+            copy = pltpu.make_async_copy(ready.at[block], out.at[place_of(block, core)], stores.at[block])
+            copy.start()
+            sent.append(copy)
+    for copy in sent:
+        copy.wait()
 
 
 def first_product(modes, table, columns, back, away):
@@ -141,9 +152,17 @@
     return pl.pallas_call(
         functools.partial(first_kernel, away),
         out_shape=jax.ShapeDtypeStruct((64, 8, width), BF16),
-        in_specs=[SMEM, VMEM, VMEM, ANY],
-        out_specs=VMEM,
-        scratch_shapes=[pltpu.VMEM((8, 64, width), BF16), DMA((8,))],
+        in_specs=[SMEM, ANY, ANY, ANY],
+        out_specs=ANY,
+        scratch_shapes=[
+            pltpu.VMEM(table.shape, F32),
+            pltpu.VMEM((2, 4, 1, 64, ORDERS), F32),
+            pltpu.VMEM((8, 64, width), BF16),
+            pltpu.VMEM((64, 8, width), BF16),
+            DMA((2,)),
+            DMA((8,)),
+            DMA((64,)),
+        ],
         compiler_params=params(60 if away else 14),
         cost_estimate=pl.CostEstimate(flops=2 << 20, bytes_accessed=4 << 20, transcendentals=0),
         name="first_away" if away else "first_keep",
@@ -162,22 +181,29 @@
             field = (row_func[block * 8 : block * 8 + 8] * col_func).astype(BF16).astype(F32)
             kept.append((mask[place, :, :cells].astype(F32) * field, mask[place, :, cells:].astype(F32) * (-field)))
         rows = slice(pair * 16, pair * 16 + 16)
+        real, imag = (jnp.concatenate([kept[0][k], kept[1][k]], axis=0) for k in range(2))
+        for keep, sign in ((plus, 1.0), (minus, -1.0)):
+            p = real[:, :half] + sign * real[:, half:]
+            q = imag[:, :half] + sign * imag[:, half:]
+            for k, part in enumerate((p + q, p, q)):
+                keep[rows, k * half : (k + 1) * half] = part.astype(BF16)
+    for n in range(2):
+        span = slice(n * 256, (n + 1) * 256)
+        sides = []
+        for keep, chirp in ((plus, even), (minus, odd)):
+            both, p, q = (
+                jnp.dot(keep[:, k * half : (k + 1) * half], chirp[k, :, span], preferred_element_type=F32)
+                for k in range(3)
+            )
+            sides.append((both + q, p - both))
         for plane in range(2):
-            both = jnp.concatenate([kept[0][plane], kept[1][plane]], axis=0)
-            span = slice(plane * half, (plane + 1) * half)
-            plus[rows, span] = (both[:, :half] + both[:, half:]).astype(BF16)
-            minus[rows, span] = (both[:, :half] - both[:, half:]).astype(BF16)
-    for n in range(4):
-        span = slice(n * 256, (n + 1) * 256)
-        e = jnp.dot(plus[...], even[:, :, :, :, span].reshape(cells, 256), preferred_element_type=F32)
-        o = jnp.dot(minus[...], odd[:, :, :, :, span].reshape(cells, 256), preferred_element_type=F32)
-        plane, at = n // 2, (n % 2) * 256
-        for shift, value in ((0, e + o), (half, e - o)):
-            value = (-value if plane else value).astype(BF16)
-            top, bottom = value[:256], value[256:]
-            where = slice(at + shift, at + shift + 256)
-            sums[plane, :, slot, :, where] = (top + bottom).reshape(4, 64, 256)
-            diffs[plane, :, slot, :, where] = (top - bottom).reshape(4, 64, 256)
+            e, o = sides[0][plane], sides[1][plane]
+            for shift, value in ((0, e + o), (half, e - o)):
+                value = value.astype(BF16)
+                top, bottom = value[:256], value[256:]
+                where = slice(n * 256 + shift, n * 256 + shift + 256)
+                sums[plane, :, slot, :, where] = (top + bottom).reshape(4, 64, 256)
+                diffs[plane, :, slot, :, where] = (top - bottom).reshape(4, 64, 256)
 
 
 def second_half(even, odd, sums, diffs, back, out, core):
@@ -207,21 +233,22 @@
 
 
 def spread_own(modes, table, columns, mask, even, odd):
-    cells = even.shape[-1]
+    cells = table.shape[-1]
     shape = jax.ShapeDtypeStruct((2, 4, 1, 64, cells), BF16)
     return pl.pallas_call(
         spread_kernel,
         out_shape=(shape, shape),
         in_specs=[SMEM] + [VMEM] * 5,
         out_specs=(VMEM, VMEM),
-        scratch_shapes=[pltpu.VMEM((512, cells), BF16)] * 2,
+        scratch_shapes=[pltpu.VMEM((512, 3 * cells // 2), BF16)] * 2,
         compiler_params=params(20),
         name="spread_own",
     )(modes, table, columns, mask, even, odd)
 
 
 def arrive_kernel(
-    modes, table, columns, mask, even, odd, own_sums, own_diffs, back, out, sums, diffs, buf, plus, minus, sem
+    modes, table, columns, mask, even, odd, left_even, left_odd, own_sums, own_diffs, back,
+    out, sums, diffs, buf, plus, minus, sem,
 ):
     core = lax.axis_index("core")
     other = 1 - core
@@ -231,22 +258,22 @@
     sums[:, :, core] = own_sums[:, :, 0]
     diffs[:, :, core] = own_diffs[:, :, 0]
     copy.wait()
-    second_half(even, odd, sums, diffs, buf, out, other)
-
-
-def arrive_away(modes, table, columns, mask, even, odd, own_sums, own_diffs, back):
+    second_half(left_even, left_odd, sums, diffs, buf, out, other)
+
+
+def arrive_away(modes, table, columns, mask, even, odd, left_even, left_odd, own_sums, own_diffs, back):
     width = back.shape[-1]
     cells = width // 2
     shape = jax.ShapeDtypeStruct((2, 4, 2, 64, cells), BF16)
     return pl.pallas_call(
         arrive_kernel,
         out_shape=(jax.ShapeDtypeStruct((64, 8, width), BF16), shape, shape),
-        in_specs=[SMEM] + [VMEM] * 7 + [ANY],
+        in_specs=[SMEM] + [VMEM] * 9 + [ANY],
         out_specs=(VMEM, VMEM, VMEM),
-        scratch_shapes=[pltpu.VMEM((2, 4, 64, width), BF16)] + [pltpu.VMEM((512, cells), BF16)] * 2 + [DMA],
-        compiler_params=params(28),
+        scratch_shapes=[pltpu.VMEM((2, 4, 64, width), BF16)] + [pltpu.VMEM((512, 3 * cells // 2), BF16)] * 2 + [DMA],
+        compiler_params=params(32),
         name="arrive_away",
-    )(modes, table, columns, mask, even, odd, own_sums, own_diffs, back)
+    )(modes, table, columns, mask, even, odd, left_even, left_odd, own_sums, own_diffs, back)
 
 
 def keep_kernel(even, odd, sums, diffs, back, out, buf, sem):
@@ -328,9 +355,11 @@
     host_table = hermite_table(cells)
     table = jnp.asarray(host_table)
     columns = jnp.asarray(host_table.T.copy()).reshape(2, 4, 2, 64, ORDERS)
-    (even_r, even_i), (odd_r, odd_i) = jax.tree.map(jnp.asarray, chirp_halves(cells))
-    even = jnp.block([[even_r, -even_i], [even_i, even_r]]).reshape(2, 4, 2, 64, cells)
-    odd = jnp.block([[odd_r, -odd_i], [odd_i, odd_r]]).reshape(2, 4, 2, 64, cells)
+    left, right = [], []
+    for r, i in chirp_halves(cells):
+        left.append(jnp.asarray(np.block([[r, -i], [i, r]])).reshape(2, 4, 2, 64, cells))
+        wide_r, wide_i = r.astype(np.float32), i.astype(np.float32)
+        right.append(jnp.asarray(np.stack([r, (wide_r + wide_i).astype(r.dtype), (wide_i - wide_r).astype(r.dtype)])))
     back_first = back_first.reshape(2, 4, 2, 64, 2 * cells)
     back_second = back_second.reshape(2, 4, 2, 64, 2 * cells)
     got = swap_cores(first_product(modes, table, columns, back_first, True))
@@ -341,10 +370,10 @@
     low, mask_first = mask_rows(near, scale_all)
     mine = exchange(low, WIDE).reshape(64, 8, width)
     other = swap_cores(mine)
-    own = spread_own(modes, table, columns, mine, even, odd)
-    away, sums, diffs = arrive_away(modes, table, columns, other, even, odd, *own, back_second)
+    own = spread_own(modes, table, columns, mine, *right)
+    away, sums, diffs = arrive_away(modes, table, columns, other, *right, *left, *own, back_second)
     got = swap_cores(away)
-    keep = arrive_keep(even, odd, sums, diffs, back_second)
+    keep = arrive_keep(*left, sums, diffs, back_second)
     partial = halve_rows((keep.astype(F32) + got.astype(F32)).astype(BF16))
     parts = exchange(partial.reshape(8, 8, width), NARROW)
     mask_second = soften(total(parts) * scale_all)

time: 129 us -> 132 us (1.023)
  Pallas kernels: 19.6 us -> 23.2 us
    pallas_call x2, Pallas kernels: 5.65 us -> 9.68 us  [first_product(): pl.pallas_call(functools.partial(first_kernel, away), out_shape=jax.Shape...]
  transfers between devices with their start and end apart: 3 -> 3, of which waited for: 3 -> 2; matrix products, arithmetic and copies ran while one was open for 0% -> 0% of each run, Pallas kernels for 6% -> 8%
where the time goes in v2:
time: 132 us
  blocking collectives  99.6 us (75%)
  Pallas kernels  23.2 us (18%)
  other arithmetic  3.07 us (2%)
  local copies, waits for them, and re-layouts  2.46 us (2%)
  waiting for transfers between devices  1.54 us (1%)
    all_to_all x5, blocking collectives, exchange(): lax.all_to_all(blocks, AXES, 0, 0, tiled=True, axis_index_groups=groups)  99.6 us
    pallas_call x2, Pallas kernels, first_product(): pl.pallas_call(functools.partial(first_kernel, away), out_shape=jax.Shape...  9.68 us
    pallas_call x1, Pallas kernels, arrive_away(): pl.pallas_call(arrive_kernel, out_shape=(jax.ShapeDtypeStruct((64, 8, wid...  6.26 us
    pallas_call x1, Pallas kernels, arrive_keep(): pl.pallas_call(keep_kernel, out_shape=jax.ShapeDtypeStruct((64, 8, width)...  3.01 us
    pallas_call x1, Pallas kernels, spread_own(): pl.pallas_call(spread_kernel, out_shape=(shape, shape), in_specs=[SMEM] +...  3.01 us
  transfers between devices with their start and end apart: 3, of which 2 were waited for; matrix products, arithmetic and copies ran while one was open for 0% of the time, Pallas kernels for 8%

profile of v2, /device:TPU:0, one launch (start us, length us, event | category | flops | bytes accessed | tf_op | source)
XLA Modules:
  0.0 131.9 jit_solution(17002018422991285031)
XLA Ops:
  0.6 0.0 copy-start.4
  0.7 4.5 %first_away.1 = bf16[64,8,2048]{2,1,0:T(8,128)(2,1)} custom-call(s32[1,2]{1,0:T(1,128)} %modes.7, f32[32,1024]{1,0:T(8,128)} %constant.16.clone.table_in.table, f32[2,4,2,64,32]{4,3,2,1,0:T(8,128)} %constant.25.columns_in.columns, bf16[2,4,2,64,2048]{4,3,2,1,0:T(8,128)(2,1)} %bitcast.15), custom_call_target="tpu_custom_call" | custom-call | flops 2097152 | bytes 4194304 | tf_op jit(solution)/shard_map/first_away/pallas_call | solution.py:152
  5.2 0.1 collective-permute-start
  5.3 2.2 %copy-done.1 = bf16[1,1024,2048]{2,1,0:T(8,128)(2,1)S(1)} copy-done((bf16[1,1024,2048]{2,1,0:T(8,128)(2,1)S(1)}, bf16[1,1024,2048]{2,1,0:T(8,128)(2,1)}, u32[]{:S(2)}) %copy-start.1) | copy-done | bytes 4194328
  7.5 5.2 %first_keep.1 = bf16[64,8,2048]{2,1,0:T(8,128)(2,1)S(1)} custom-call(s32[1,2]{1,0:T(1,128)S(1)} %copy-done.8, f32[32,1024]{1,0:T(8,128)S(1)} %copy-done.7, f32[2,4,2,64,32]{4,3,2,1,0:T(8,128)S(1)} %copy-done.4, bf16[2,4,2,64,2048]{4,3,2,1,0:T(8,128)(2,1)S(1)} %bitcast.16), custom_call_target="tpu_custom_call" | custom-call | flops 2097152 | bytes 4194304 | tf_op jit(solution)/shard_map/first_keep/pallas_call | solution.py:152
  12.7 0.9 add_convert_fusion.1
  13.6 21.5 %all_to_all.25 = bf16[8,64,2048]{2,1,0:T(8,128)(2,1)S(1)} all-to-all(bf16[8,64,2048]{2,1,0:T(8,128)(2,1)S(1)} %bitcast.19), channel_id=1, replica_groups={{0,16,1,17,2,18,3,19},{48,32,49,33,50,34,51,35},{65,81,64,80,67,83,66,8..., dimensions={0} | all-to-all | bytes 4194304 | tf_op jit(solution)/shard_map/all_to_all | solution.py:301
  35.1 0.3 fusion
  35.4 0.2 broadcast_in_dim.9
  35.7 27.4 %all_to_all.26.near = bf16[8,64,2048]{2,1,0:T(8,128)(2,1)S(1)} all-to-all(bf16[8,64,2048]{2,1,0:T(8,128)(2,1)S(1)} %broadcast_in_dim.9), channel_id=1, replica_groups={{0,48,65,113,6,54,71,119},{16,32,81,97,22,38,87,103},{1,49,64,112,7,55,..., dimensions={0} | all-to-all | bytes 4194304 | tf_op jit(solution)/shard_map/all_to_all | solution.py:301
  63.0 1.3 mask_rows.1
  64.3 19.1 %all_to_all.27 = bf16[8,64,2048]{2,1,0:T(8,128)(2,1)S(1)} all-to-all(bf16[8,64,2048]{2,1,0:T(8,128)(2,1)S(1)} %get-tuple-element.10), channel_id=1, replica_groups={{0,16,1,17,2,18,3,19},{48,32,49,33,50,34,51,35},{65,81,64,80,67,83,66,8..., dimensions={0} | all-to-all | bytes 4194304 | tf_op jit(solution)/shard_map/all_to_all | solution.py:301
  83.5 0.7 collective-permute-start.1
  84.1 3.0 %spread_own.1 = (bf16[2,4,1,64,1024]{4,3,2,1,0:T(8,128)(2,1)S(1)}, bf16[2,4,1,64,1024]{4,3,2,1,0:T(8,128)(2,1)S(1)}) custom-call(s32[1,2]{1,0:T(1,128)S(1)} %copy-done.8, f32[32,1024]{1,0:T(8,128)S(1)} %copy-done.7, f32[2,4,2,64,32]{4,3,2,1,0:T(8,128)S(1)} %copy-done.4, bf16[64,8,2048]{2,1,0:T(8,128)(2,1)S(1)} %bitcast.18, ...), custom_call_target="tpu_custom_call" | custom-call | tf_op jit(solution)/shard_map/spread_own/pallas_call | solution.py:238
  87.2 0.8 collective-permute-done.1.mask
  87.9 6.3 %arrive_away.1 = (bf16[64,8,2048]{2,1,0:T(8,128)(2,1)S(1)}, bf16[2,4,2,64,1024]{4,3,2,1,0:T(8,128)(2,1)S(1)}, bf16[2,4,2,64,1024]{4,3,2,1,0:T(8,128)(2,1)S(1)}) custom-call(s32[1,2]{1,0:T(1,128)S(1)} %copy-done.8, f32[32,1024]{1,0:T(8,128)S(1)} %copy-done.7, f32[2,4,2,64,32]{4,3,2,1,0:T(8,128)S(1)} %copy-done.4, ...), custom_call_target="tpu_custom_call" | custom-call | tf_op jit(solution)/shard_map/arrive_away/pallas_call | solution.py:268
  94.2 0.5 collective-permute-start.2
  94.7 3.0 %arrive_keep.1 = bf16[64,8,2048]{2,1,0:T(8,128)(2,1)S(1)} custom-call(bf16[2,4,2,64,1024]{4,3,2,1,0:T(8,128)(2,1)S(1)} %copy-done.3, bf16[2,4,2,64,1024]{4,3,2,1,0:T(8,128)(2,1)S(1)} %copy-done.2, bf16[2,4,2,64,1024]{4,3,2,1,0:T(8,128)(2,1)S(1)} %get-tuple-element.13.sums, bf16[2,4,2,64,1024]{4,3,2,1,0:T(8,128)(2,1)S(1)} %get-tuple-element.14.diffs, ...), custom_call_target="tpu_custom_call" | custom-call | tf_op jit(solution)/shard_map/arrive_keep/pallas_call | solution.py:289
  97.7 0.8 collective-permute-done.2
  98.5 0.8 add_convert_fusion
  99.2 18.9 %all_to_all.28 = bf16[8,64,2048]{2,1,0:T(8,128)(2,1)S(1)} all-to-all(bf16[8,64,2048]{2,1,0:T(8,128)(2,1)S(1)} %bitcast.20), channel_id=1, replica_groups={{0,16,1,17,2,18,3,19},{48,32,49,33,50,34,51,35},{65,81,64,80,67,83,66,8..., dimensions={0} | all-to-all | bytes 4194304 | tf_op jit(solution)/shard_map/all_to_all | solution.py:301
  118.1 0.3 fusion.1
  118.5 12.7 %all_to_all.29 = bf16[8,8,2048]{2,1,0:T(8,128)(2,1)S(1)} all-to-all(bf16[8,8,2048]{2,1,0:T(8,128)(2,1)S(1)} %fusion.1), channel_id=1, replica_groups={{0,48,65,113,6,54,71,119},{16,32,81,97,22,38,87,103},{1,49,64,112,7,55,..., dimensions={0} | all-to-all | bytes 524288 | tf_op jit(solution)/shard_map/all_to_all | solution.py:301
  131.2 0.7 maximum_divide_fusion
  (19 shorter events, 0.1 us)
Async XLA Ops:
  0.6 4.6 %copy-start.4 = (f32[2,4,2,64,32]{4,3,2,1,0:T(8,128)S(1)}, f32[2,4,2,64,32]{4,3,2,1,0:T(8,128)}, u32[]{:S(2)}) copy-start(f32[2,4,2,64,32]{4,3,2,1,0:T(8,128)} %constant.25.columns_in.columns) | copy-start | bytes 393220
  0.6 4.6 %copy-start.7 = (f32[32,1024]{1,0:T(8,128)S(1)}, f32[32,1024]{1,0:T(8,128)}, u32[]{:S(2)}) copy-start(f32[32,1024]{1,0:T(8,128)} %constant.16.clone.table_in.table) | copy-start | bytes 393220
  0.7 4.6 %copy-start.8 = (s32[1,2]{1,0:T(1,128)S(1)}, s32[1,2]{1,0:T(1,128)}, u32[]{:S(2)}) copy-start(s32[1,2]{1,0:T(1,128)} %modes.7) | copy-start | bytes 28
  5.2 7.5 %collective-permute-start = (bf16[64,8,2048]{2,1,0:T(8,128)(2,1)}, bf16[64,8,2048]{2,1,0:T(8,128)(2,1)S(1)}, u32[]{:S(2)}, u32[]{:S(2)}) collective-permute-start(bf16[64,8,2048]{2,1,0:T(8,128)(2,1)} %first_away.1), channel_id=1, source_target_pairs={{0,8},{8,0},{1,9},{9,1},{2,10},{10,2},{3,11},{11,3},{4,12},{12,4},... | collective-permute-start | bytes 6291464 | tf_op jit(solution)/shard_map/ppermute | solution.py:71
  5.3 2.2 %copy-start.1 = (bf16[1,1024,2048]{2,1,0:T(8,128)(2,1)S(1)}, bf16[1,1024,2048]{2,1,0:T(8,128)(2,1)}, u32[]{:S(2)}) copy-start(bf16[1,1024,2048]{2,1,0:T(8,128)(2,1)} %param.10) | copy-start | bytes 12582916
  63.0 21.1 %copy-start.5 = (bf16[3,512,512]{2,1,0:T(8,128)(2,1)S(1)}, bf16[3,512,512]{2,1,0:T(8,128)(2,1)}, u32[]{:S(2)}) copy-start(bf16[3,512,512]{2,1,0:T(8,128)(2,1)} %constant.21.clone.odd) | copy-start | bytes 4718596
  63.0 21.1 %copy-start.6 = (bf16[3,512,512]{2,1,0:T(8,128)(2,1)S(1)}, bf16[3,512,512]{2,1,0:T(8,128)(2,1)}, u32[]{:S(2)}) copy-start(bf16[3,512,512]{2,1,0:T(8,128)(2,1)} %constant.19.clone.even) | copy-start | bytes 4718596
  64.3 23.6 %copy-start.2 = (bf16[2,4,2,64,1024]{4,3,2,1,0:T(8,128)(2,1)S(1)}, bf16[2,4,2,64,1024]{4,3,2,1,0:T(8,128)(2,1)}, u32[]{:S(2)}) copy-start(bf16[2,4,2,64,1024]{4,3,2,1,0:T(8,128)(2,1)} %constant.27.left_odd.odd) | copy-start | bytes 6291460
  64.3 23.6 %copy-start.3 = (bf16[2,4,2,64,1024]{4,3,2,1,0:T(8,128)(2,1)S(1)}, bf16[2,4,2,64,1024]{4,3,2,1,0:T(8,128)(2,1)}, u32[]{:S(2)}) copy-start(bf16[2,4,2,64,1024]{4,3,2,1,0:T(8,128)(2,1)} %constant.26.left_even.even) | copy-start | bytes 6291460
  83.5 4.5 %copy-start = (bf16[1,1024,2048]{2,1,0:T(8,128)(2,1)S(1)}, bf16[1,1024,2048]{2,1,0:T(8,128)(2,1)}, u32[]{:S(2)}) copy-start(bf16[1,1024,2048]{2,1,0:T(8,128)(2,1)} %param.11) | copy-start | bytes 12582916
  83.5 4.5 %collective-permute-start.1 = (bf16[64,8,2048]{2,1,0:T(8,128)(2,1)S(1)}, bf16[64,8,2048]{2,1,0:T(8,128)(2,1)S(1)}, u32[]{:S(2)}, u32[]{:S(2)}) collective-permute-start(bf16[64,8,2048]{2,1,0:T(8,128)(2,1)S(1)} %bitcast.17), channel_id=1, source_target_pairs={{0,8},{8,0},{1,9},{9,1},{2,10},{10,2},{3,11},{11,3},{4,12},{12,4},... | collective-permute-start | bytes 6291464 | tf_op jit(solution)/shard_map/ppermute | solution.py:71
  94.2 4.2 %collective-permute-start.2 = (bf16[64,8,2048]{2,1,0:T(8,128)(2,1)S(1)}, bf16[64,8,2048]{2,1,0:T(8,128)(2,1)S(1)}, u32[]{:S(2)}, u32[]{:S(2)}) collective-permute-start(bf16[64,8,2048]{2,1,0:T(8,128)(2,1)S(1)} %get-tuple-element.15), channel_id=1, source_target_pairs={{0,8},{8,0},{1,9},{9,1},{2,10},{10,2},{3,11},{11,3},{4,12},{12,4},... | collective-permute-start | bytes 6291464 | tf_op jit(solution)/shard_map/ppermute | solution.py:71

commit v3 on v1

--- a/solution.py
+++ b/solution.py
@@ -113,16 +113,22 @@
 WIDE, NARROW = device_groups()
 
 
-def first_kernel(away, modes, table, columns, back, out, buf, sems):
+def first_kernel(away, modes, table_in, columns_in, back, out, table, columns, buf, loads, sems):
     core = lax.axis_index("core")
     if away:
         core = 1 - core
+    heads = [
+        pltpu.make_async_copy(table_in, table, loads.at[0]),
+        pltpu.make_async_copy(columns_in.at[:, :, core], columns.at[:, :, 0], loads.at[1]),
+    ]
     copies = [
         pltpu.make_async_copy(back.at[k // 4, k % 4, core], buf.at[k], sems.at[k]) for k in range(8)
     ]
-    for copy in copies:
+    for copy in heads + copies:
         copy.start()
-    row_func = row_of(modes, columns, core)
+    for copy in heads:
+        copy.wait()
+    row_func = row_of(modes, columns, 0)
     col_func = table[pl.ds(modes[0, 1], 1), :]
     cells = col_func.shape[1]
     for k in range(8):
@@ -130,10 +136,10 @@
         for j in range(8):
             block = k * 8 + j
             place = place_of(block, core)
-            field = (row_func[block * 8 : block * 8 + 8] * col_func).astype(BF16).astype(F32)
+            field = (row_func[block * 8 : block * 8 + 8] * col_func).astype(BF16)
             for plane in range(2):
                 span = slice(plane * cells, (plane + 1) * cells)
-                out[place, :, span] = (buf[k, j * 8 : j * 8 + 8, span].astype(F32) * field).astype(BF16)
+                out[place, :, span] = buf[k, j * 8 : j * 8 + 8, span] * field
 
 
 def first_product(modes, table, columns, back, away):
@@ -141,9 +147,15 @@
     return pl.pallas_call(
         functools.partial(first_kernel, away),
         out_shape=jax.ShapeDtypeStruct((64, 8, width), BF16),
-        in_specs=[SMEM, VMEM, VMEM, ANY],
+        in_specs=[SMEM, ANY, ANY, ANY],
         out_specs=VMEM,
-        scratch_shapes=[pltpu.VMEM((8, 64, width), BF16), DMA((8,))],
+        scratch_shapes=[
+            pltpu.VMEM(table.shape, F32),
+            pltpu.VMEM((2, 4, 1, 64, ORDERS), F32),
+            pltpu.VMEM((8, 64, width), BF16),
+            DMA((2,)),
+            DMA((8,)),
+        ],
         compiler_params=params(60 if away else 14),
         cost_estimate=pl.CostEstimate(flops=2 << 20, bytes_accessed=4 << 20, transcendentals=0),
         name="first_away" if away else "first_keep",
@@ -156,17 +168,14 @@
     cells = col_func.shape[1]
     half = cells // 2
     for pair in range(32):
-        kept = []
-        for block in (2 * pair, 2 * pair + 1):
-            place = place_of(block, core)
-            field = (row_func[block * 8 : block * 8 + 8] * col_func).astype(BF16).astype(F32)
-            kept.append((mask[place, :, :cells].astype(F32) * field, mask[place, :, cells:].astype(F32) * (-field)))
+        first, second = (mask[place_of(2 * pair + k, core)] for k in range(2))
+        both = jnp.concatenate([first, second], axis=0)
         rows = slice(pair * 16, pair * 16 + 16)
-        for plane in range(2):
-            both = jnp.concatenate([kept[0][plane], kept[1][plane]], axis=0)
+        field = (row_func[rows] * col_func).astype(BF16)
+        for plane, value in ((0, both[:, :cells] * field), (1, both[:, cells:] * (-field))):
             span = slice(plane * half, (plane + 1) * half)
-            plus[rows, span] = (both[:, :half] + both[:, half:]).astype(BF16)
-            minus[rows, span] = (both[:, :half] - both[:, half:]).astype(BF16)
+            plus[rows, span] = value[:, :half] + value[:, half:]
+            minus[rows, span] = value[:, :half] - value[:, half:]
     for n in range(4):
         span = slice(n * 256, (n + 1) * 256)
         e = jnp.dot(plus[...], even[:, :, :, :, span].reshape(cells, 256), preferred_element_type=F32)
@@ -186,19 +195,23 @@
     rows_odd = odd[:, :, core].reshape(512, cells)
     for n in range(4):
         span = slice(n * 256, (n + 1) * 256)
-        e = jnp.dot(rows_even, sums[:, :, :, :, span].reshape(cells, 256), preferred_element_type=F32)
-        o = jnp.dot(rows_odd, diffs[:, :, :, :, span].reshape(cells, 256), preferred_element_type=F32)
         other = slice(cells + n * 256, cells + (n + 1) * 256)
-        for h, value in ((0, e + o), (1, e - o)):
-            real, imag = value[:256], value[256:]
-            back_real = back[h, :, :, span].reshape(256, 256).astype(F32)
-            back_imag = back[h, :, :, other].reshape(256, 256).astype(F32)
-            new_real = back_real * real + back_imag * imag
-            new_imag = back_imag * real - back_real * imag
-            for j in range(32):
+        right_even = sums[:, :, :, :, span].reshape(cells, 256)
+        right_odd = diffs[:, :, :, :, span].reshape(cells, 256)
+        e, o = (
+            [jnp.dot(rows[k * 256 : k * 256 + 256], right, preferred_element_type=F32) for k in range(2)]
+            for rows, right in ((rows_even, right_even), (rows_odd, right_odd))
+        )
+        for j in range(32):
+            for h in range(2):
+                at = slice(j * 8, j * 8 + 8)
+                real = e[0][at] - o[0][at] if h else e[0][at] + o[0][at]
+                imag = e[1][at] - o[1][at] if h else e[1][at] + o[1][at]
+                back_real = back[h, j // 8, j % 8 * 8 : j % 8 * 8 + 8, span].astype(F32)
+                back_imag = back[h, j // 8, j % 8 * 8 : j % 8 * 8 + 8, other].astype(F32)
                 place = place_of(h * 32 + j, core)
-                out[place, :, span] = new_real[j * 8 : j * 8 + 8].astype(BF16)
-                out[place, :, other] = new_imag[j * 8 : j * 8 + 8].astype(BF16)
+                out[place, :, span] = (back_real * real + back_imag * imag).astype(BF16)
+                out[place, :, other] = (back_imag * real - back_real * imag).astype(BF16)
 
 
 def spread_kernel(modes, table, columns, mask, even, odd, sums, diffs, plus, minus):

time: 129 us -> 128 us (level)
  no operation moved by 1% of the time
where the time goes in v3:
time: 128 us
  blocking collectives  99.6 us (78%)
  Pallas kernels  18.8 us (15%)
  other arithmetic  3.06 us (2%)
  local copies, waits for them, and re-layouts  2.45 us (2%)
  waiting for transfers between devices  2.43 us (2%)
    all_to_all x5, blocking collectives, exchange(): lax.all_to_all(blocks, AXES, 0, 0, tiled=True, axis_index_groups=groups)  99.6 us
    pallas_call x1, Pallas kernels, arrive_away(): pl.pallas_call(arrive_kernel, out_shape=(jax.ShapeDtypeStruct((64, 8, wid...  6.08 us
    pallas_call x2, Pallas kernels, first_product(): pl.pallas_call(functools.partial(first_kernel, away), out_shape=jax.Shape...  5.48 us
    pallas_call x1, Pallas kernels, arrive_keep(): pl.pallas_call(keep_kernel, out_shape=jax.ShapeDtypeStruct((64, 8, width)...  2.99 us
    pallas_call x1, Pallas kernels, spread_own(): pl.pallas_call(spread_kernel, out_shape=(shape, shape), in_specs=[SMEM] +...  2.99 us
  transfers between devices with their start and end apart: 3, of which 3 were waited for; matrix products, arithmetic and copies ran while one was open for 0% of the time, Pallas kernels for 6%

profile of v3, /device:TPU:0, one launch (start us, length us, event | category | flops | bytes accessed | tf_op | source)
XLA Modules:
  0.0 128.1 jit_solution(326132327795684774)
XLA Ops:
  0.7 4.1 %first_away.1 = bf16[64,8,2048]{2,1,0:T(8,128)(2,1)} custom-call(s32[1,2]{1,0:T(1,128)} %modes.7, f32[32,1024]{1,0:T(8,128)} %constant.16.clone.table_in.table, f32[2,4,2,64,32]{4,3,2,1,0:T(8,128)} %constant.25.columns_in.columns, bf16[2,4,2,64,2048]{4,3,2,1,0:T(8,128)(2,1)} %bitcast.15), custom_call_target="tpu_custom_call" | custom-call | flops 2097152 | bytes 4194304 | tf_op jit(solution)/shard_map/first_away/pallas_call | solution.py:147
  4.8 0.1 collective-permute-start
  4.9 2.2 %copy-done.3 = bf16[1,1024,2048]{2,1,0:T(8,128)(2,1)S(1)} copy-done((bf16[1,1024,2048]{2,1,0:T(8,128)(2,1)S(1)}, bf16[1,1024,2048]{2,1,0:T(8,128)(2,1)}, u32[]{:S(2)}) %copy-start.3) | copy-done | bytes 4194328
  7.1 1.3 %first_keep.1 = bf16[64,8,2048]{2,1,0:T(8,128)(2,1)S(1)} custom-call(s32[1,2]{1,0:T(1,128)S(1)} %copy-done.6, f32[32,1024]{1,0:T(8,128)S(1)} %copy-done.5, f32[2,4,2,64,32]{4,3,2,1,0:T(8,128)S(1)} %copy-done.4, bf16[2,4,2,64,2048]{4,3,2,1,0:T(8,128)(2,1)S(1)} %bitcast.16), custom_call_target="tpu_custom_call" | custom-call | flops 2097152 | bytes 4194304 | tf_op jit(solution)/shard_map/first_keep/pallas_call | solution.py:147
  8.5 0.8 collective-permute-done
  9.3 0.9 add_convert_fusion.1
  10.2 21.5 %all_to_all.25 = bf16[8,64,2048]{2,1,0:T(8,128)(2,1)S(1)} all-to-all(bf16[8,64,2048]{2,1,0:T(8,128)(2,1)S(1)} %bitcast.19), channel_id=1, replica_groups={{0,16,1,17,2,18,3,19},{48,32,49,33,50,34,51,35},{65,81,64,80,67,83,66,8..., dimensions={0} | all-to-all | bytes 4194304 | tf_op jit(solution)/shard_map/all_to_all | solution.py:287
  31.7 0.3 fusion
  32.0 0.2 broadcast_in_dim.9
  32.2 27.4 %all_to_all.26.near = bf16[8,64,2048]{2,1,0:T(8,128)(2,1)S(1)} all-to-all(bf16[8,64,2048]{2,1,0:T(8,128)(2,1)S(1)} %broadcast_in_dim.9), channel_id=1, replica_groups={{0,48,65,113,6,54,71,119},{16,32,81,97,22,38,87,103},{1,49,64,112,7,55,..., dimensions={0} | all-to-all | bytes 4194304 | tf_op jit(solution)/shard_map/all_to_all | solution.py:287
  59.6 1.3 mask_rows.1
  60.9 19.1 %all_to_all.27 = bf16[8,64,2048]{2,1,0:T(8,128)(2,1)S(1)} all-to-all(bf16[8,64,2048]{2,1,0:T(8,128)(2,1)S(1)} %get-tuple-element.10), channel_id=1, replica_groups={{0,16,1,17,2,18,3,19},{48,32,49,33,50,34,51,35},{65,81,64,80,67,83,66,8..., dimensions={0} | all-to-all | bytes 4194304 | tf_op jit(solution)/shard_map/all_to_all | solution.py:287
  80.0 0.3 collective-permute-start.1
  80.4 3.0 %spread_own.1 = (bf16[2,4,1,64,1024]{4,3,2,1,0:T(8,128)(2,1)S(1)}, bf16[2,4,1,64,1024]{4,3,2,1,0:T(8,128)(2,1)S(1)}) custom-call(s32[1,2]{1,0:T(1,128)S(1)} %copy-done.6, f32[32,1024]{1,0:T(8,128)S(1)} %copy-done.5, f32[2,4,2,64,32]{4,3,2,1,0:T(8,128)S(1)} %copy-done.4, bf16[64,8,2048]{2,1,0:T(8,128)(2,1)S(1)} %bitcast.18, ...), custom_call_target="tpu_custom_call" | custom-call | tf_op jit(solution)/shard_map/spread_own/pallas_call | solution.py:225
  83.4 0.8 collective-permute-done.1.mask
  84.2 6.1 %arrive_away.1 = (bf16[64,8,2048]{2,1,0:T(8,128)(2,1)S(1)}, bf16[2,4,2,64,1024]{4,3,2,1,0:T(8,128)(2,1)S(1)}, bf16[2,4,2,64,1024]{4,3,2,1,0:T(8,128)(2,1)S(1)}) custom-call(s32[1,2]{1,0:T(1,128)S(1)} %copy-done.6, f32[32,1024]{1,0:T(8,128)S(1)} %copy-done.5, f32[2,4,2,64,32]{4,3,2,1,0:T(8,128)S(1)} %copy-done.4, ...), custom_call_target="tpu_custom_call" | custom-call | tf_op jit(solution)/shard_map/arrive_away/pallas_call | solution.py:254
  90.3 0.6 collective-permute-start.2
  90.9 3.0 %arrive_keep.1 = bf16[64,8,2048]{2,1,0:T(8,128)(2,1)S(1)} custom-call(bf16[2,4,2,64,1024]{4,3,2,1,0:T(8,128)(2,1)S(1)} %copy-done.1, bf16[2,4,2,64,1024]{4,3,2,1,0:T(8,128)(2,1)S(1)} %copy-done, bf16[2,4,2,64,1024]{4,3,2,1,0:T(8,128)(2,1)S(1)} %get-tuple-element.13.sums, bf16[2,4,2,64,1024]{4,3,2,1,0:T(8,128)(2,1)S(1)} %get-tuple-element.14.diffs, ...), custom_call_target="tpu_custom_call" | custom-call | tf_op jit(solution)/shard_map/arrive_keep/pallas_call | solution.py:275
  93.9 0.8 collective-permute-done.2
  94.7 0.8 add_convert_fusion
  95.5 18.9 %all_to_all.28 = bf16[8,64,2048]{2,1,0:T(8,128)(2,1)S(1)} all-to-all(bf16[8,64,2048]{2,1,0:T(8,128)(2,1)S(1)} %bitcast.20), channel_id=1, replica_groups={{0,16,1,17,2,18,3,19},{48,32,49,33,50,34,51,35},{65,81,64,80,67,83,66,8..., dimensions={0} | all-to-all | bytes 4194304 | tf_op jit(solution)/shard_map/all_to_all | solution.py:287
  114.4 0.3 fusion.1
  114.7 12.7 %all_to_all.29 = bf16[8,8,2048]{2,1,0:T(8,128)(2,1)S(1)} all-to-all(bf16[8,8,2048]{2,1,0:T(8,128)(2,1)S(1)} %fusion.1), channel_id=1, replica_groups={{0,48,65,113,6,54,71,119},{16,32,81,97,22,38,87,103},{1,49,64,112,7,55,..., dimensions={0} | all-to-all | bytes 524288 | tf_op jit(solution)/shard_map/all_to_all | solution.py:287
  127.5 0.7 maximum_divide_fusion
  (15 shorter events, 0.1 us)
Async XLA Ops:
  0.6 4.3 %copy-start.4 = (f32[2,4,2,64,32]{4,3,2,1,0:T(8,128)S(1)}, f32[2,4,2,64,32]{4,3,2,1,0:T(8,128)}, u32[]{:S(2)}) copy-start(f32[2,4,2,64,32]{4,3,2,1,0:T(8,128)} %constant.25.columns_in.columns) | copy-start | bytes 393220
  0.6 4.3 %copy-start.5 = (f32[32,1024]{1,0:T(8,128)S(1)}, f32[32,1024]{1,0:T(8,128)}, u32[]{:S(2)}) copy-start(f32[32,1024]{1,0:T(8,128)} %constant.16.clone.table_in.table) | copy-start | bytes 393220
  0.7 4.3 %copy-start.6 = (s32[1,2]{1,0:T(1,128)S(1)}, s32[1,2]{1,0:T(1,128)}, u32[]{:S(2)}) copy-start(s32[1,2]{1,0:T(1,128)} %modes.7) | copy-start | bytes 28
  4.8 4.5 %collective-permute-start = (bf16[64,8,2048]{2,1,0:T(8,128)(2,1)}, bf16[64,8,2048]{2,1,0:T(8,128)(2,1)S(1)}, u32[]{:S(2)}, u32[]{:S(2)}) collective-permute-start(bf16[64,8,2048]{2,1,0:T(8,128)(2,1)} %first_away.1), channel_id=1, source_target_pairs={{0,8},{8,0},{1,9},{9,1},{2,10},{10,2},{3,11},{11,3},{4,12},{12,4},... | collective-permute-start | bytes 6291464 | tf_op jit(solution)/shard_map/ppermute | solution.py:71
  4.9 2.2 %copy-start.3 = (bf16[1,1024,2048]{2,1,0:T(8,128)(2,1)S(1)}, bf16[1,1024,2048]{2,1,0:T(8,128)(2,1)}, u32[]{:S(2)}) copy-start(bf16[1,1024,2048]{2,1,0:T(8,128)(2,1)} %param.10) | copy-start | bytes 12582916
  60.9 19.5 %copy-start = (bf16[2,4,2,64,1024]{4,3,2,1,0:T(8,128)(2,1)S(1)}, bf16[2,4,2,64,1024]{4,3,2,1,0:T(8,128)(2,1)}, u32[]{:S(2)}) copy-start(bf16[2,4,2,64,1024]{4,3,2,1,0:T(8,128)(2,1)} %constant.35.odd) | copy-start | bytes 6291460
  60.9 19.5 %copy-start.1 = (bf16[2,4,2,64,1024]{4,3,2,1,0:T(8,128)(2,1)S(1)}, bf16[2,4,2,64,1024]{4,3,2,1,0:T(8,128)(2,1)}, u32[]{:S(2)}) copy-start(bf16[2,4,2,64,1024]{4,3,2,1,0:T(8,128)(2,1)} %constant.30.even) | copy-start | bytes 6291460
  80.0 4.2 %copy-start.2 = (bf16[1,1024,2048]{2,1,0:T(8,128)(2,1)S(1)}, bf16[1,1024,2048]{2,1,0:T(8,128)(2,1)}, u32[]{:S(2)}) copy-start(bf16[1,1024,2048]{2,1,0:T(8,128)(2,1)} %param.11) | copy-start | bytes 12582916
  80.0 4.2 %collective-permute-start.1 = (bf16[64,8,2048]{2,1,0:T(8,128)(2,1)S(1)}, bf16[64,8,2048]{2,1,0:T(8,128)(2,1)S(1)}, u32[]{:S(2)}, u32[]{:S(2)}) collective-permute-start(bf16[64,8,2048]{2,1,0:T(8,128)(2,1)S(1)} %bitcast.17), channel_id=1, source_target_pairs={{0,8},{8,0},{1,9},{9,1},{2,10},{10,2},{3,11},{11,3},{4,12},{12,4},... | collective-permute-start | bytes 6291464 | tf_op jit(solution)/shard_map/ppermute | solution.py:71
  90.3 4.4 %collective-permute-start.2 = (bf16[64,8,2048]{2,1,0:T(8,128)(2,1)S(1)}, bf16[64,8,2048]{2,1,0:T(8,128)(2,1)S(1)}, u32[]{:S(2)}, u32[]{:S(2)}) collective-permute-start(bf16[64,8,2048]{2,1,0:T(8,128)(2,1)S(1)} %get-tuple-element.15), channel_id=1, source_target_pairs={{0,8},{8,0},{1,9},{9,1},{2,10},{10,2},{3,11},{11,3},{4,12},{12,4},... | collective-permute-start | bytes 6291464 | tf_op jit(solution)/shard_map/ppermute | solution.py:71

commit v4 on v3

--- a/solution.py
+++ b/solution.py
@@ -113,53 +113,64 @@
 WIDE, NARROW = device_groups()
 
 
-def first_kernel(away, modes, table_in, columns_in, back, out, table, columns, buf, loads, sems):
-    core = lax.axis_index("core")
-    if away:
-        core = 1 - core
-    heads = [
-        pltpu.make_async_copy(table_in, table, loads.at[0]),
-        pltpu.make_async_copy(columns_in.at[:, :, core], columns.at[:, :, 0], loads.at[1]),
-    ]
+def own_kernel(modes, table, columns, back, out, buf, sems):
+    core = lax.axis_index("core")
     copies = [
         pltpu.make_async_copy(back.at[k // 4, k % 4, core], buf.at[k], sems.at[k]) for k in range(8)
     ]
-    for copy in heads + copies:
+    for copy in copies:
         copy.start()
-    for copy in heads:
-        copy.wait()
-    row_func = row_of(modes, columns, 0)
+    row_func = row_of(modes, columns, core)
     col_func = table[pl.ds(modes[0, 1], 1), :]
-    cells = col_func.shape[1]
+    cells = table.shape[1]
     for k in range(8):
         copies[k].wait()
         for j in range(8):
             block = k * 8 + j
-            place = place_of(block, core)
             field = (row_func[block * 8 : block * 8 + 8] * col_func).astype(BF16)
             for plane in range(2):
                 span = slice(plane * cells, (plane + 1) * cells)
-                out[place, :, span] = buf[k, j * 8 : j * 8 + 8, span] * field
-
-
-def first_product(modes, table, columns, back, away):
+                out[place_of(block, core), :, span] = buf[k, j * 8 : j * 8 + 8, span] * field
+
+
+def own_product(modes, table, columns, back):
     width = back.shape[-1]
     return pl.pallas_call(
-        functools.partial(first_kernel, away),
+        own_kernel,
         out_shape=jax.ShapeDtypeStruct((64, 8, width), BF16),
-        in_specs=[SMEM, ANY, ANY, ANY],
+        in_specs=[SMEM, VMEM, VMEM, ANY],
         out_specs=VMEM,
-        scratch_shapes=[
-            pltpu.VMEM(table.shape, F32),
-            pltpu.VMEM((2, 4, 1, 64, ORDERS), F32),
-            pltpu.VMEM((8, 64, width), BF16),
-            DMA((2,)),
-            DMA((8,)),
-        ],
-        compiler_params=params(60 if away else 14),
+        scratch_shapes=[pltpu.VMEM((8, 64, width), BF16), DMA((8,))],
+        compiler_params=params(14),
         cost_estimate=pl.CostEstimate(flops=2 << 20, bytes_accessed=4 << 20, transcendentals=0),
-        name="first_away" if away else "first_keep",
+        name="own_product",
     )(modes, table, columns, back)
+
+
+def both_kernel(peer, table, columns, got, keep, out):
+    core = lax.axis_index("core")
+    row_func = row_of(peer, columns, core)
+    col_func = table[pl.ds(peer[0, 1], 1), :]
+    cells = table.shape[1]
+    for block in range(64):
+        place = place_of(block, core)
+        k, j = block // 8, block % 8
+        field = (row_func[block * 8 : block * 8 + 8] * col_func).astype(BF16).astype(F32)
+        for plane in range(2):
+            span = slice(plane * cells, (plane + 1) * cells)
+            value = got[k // 4, k % 4, j * 8 : j * 8 + 8, span].astype(F32) * field
+            out[place, :, span] = (value + keep[place, :, span].astype(F32)).astype(BF16)
+
+
+def both_products(peer, table, columns, got, keep):
+    return pl.pallas_call(
+        both_kernel,
+        out_shape=jax.ShapeDtypeStruct(keep.shape, BF16),
+        in_specs=[SMEM] + [VMEM] * 4,
+        out_specs=VMEM,
+        compiler_params=params(14),
+        name="both_products",
+    )(peer, table, columns, got, keep)
 
 
 def spread_half(modes, table, columns, mask, even, odd, plus, minus, sums, diffs, core, slot):
@@ -312,9 +323,9 @@
         rows = slice(block * 8, block * 8 + 8)
         real = total([near[k, rows, :cells] for k in range(8)]) * scale
         imag = total([near[k, rows, cells:] for k in range(8)]) * scale
-        size = jnp.sqrt(real * real + imag * imag + 1.0)
+        inverse = 1.0 / jnp.sqrt(real * real + imag * imag + 1.0)
         for span, part in ((slice(0, cells), real), (slice(cells, 2 * cells), imag)):
-            part = part / size
+            part = part * inverse
             every[block, :, span] = part
             part = part.astype(BF16)
             for k in range(8):
@@ -346,9 +357,11 @@
     odd = jnp.block([[odd_r, -odd_i], [odd_i, odd_r]]).reshape(2, 4, 2, 64, cells)
     back_first = back_first.reshape(2, 4, 2, 64, 2 * cells)
     back_second = back_second.reshape(2, 4, 2, 64, 2 * cells)
-    got = swap_cores(first_product(modes, table, columns, back_first, True))
-    keep = first_product(modes, table, columns, back_first, False)
-    partial = halve_rows((keep.astype(F32) + got.astype(F32)).astype(BF16))
+    peer = swap_cores(modes)
+    away = lax.dynamic_index_in_dim(back_first, 1 - lax.axis_index("core"), 2, keepdims=False)
+    got = swap_cores(away)
+    keep = own_product(modes, table, columns, back_first)
+    partial = halve_rows(both_products(peer, table, columns, got, keep))
     width = 2 * cells
     near = exchange(jnp.broadcast_to(partial[None], (8, 64, width)), NARROW)
     low, mask_first = mask_rows(near, scale_all)

time: 128 us -> 127 us (level)
  Pallas kernels: 18.8 us -> 15.9 us
  local copies, waits for them, and re-layouts: 2.45 us -> 4.43 us
    pallas_call x2, Pallas kernels: 5.48 us -> 2.58 us  [the longest x1 1.45 us: both_products(): pl.pallas_call(both_kernel, out_shape=jax.ShapeDtypeStruct(keep.shape, BF...]
    squeeze x0 -> x1, local copies, waits for them, and re-layouts: none -> 1.89 us  [body(): lax.dynamic_index_in_dim(back_first, 1 - lax.axis_index('core'), 2, keepd...]
  transfers between devices with their start and end apart: 3 -> 4, of which waited for: 3 -> 3; matrix products, arithmetic and copies ran while one was open for 0% -> 0% of each run, Pallas kernels for 6% -> 6%
where the time goes in v4:
time: 127 us; the launch traced here: 126 us
  blocking collectives  99.6 us (78%)
  Pallas kernels  15.9 us (13%)
  local copies, waits for them, and re-layouts  4.43 us (3%)
  other arithmetic  2.16 us (2%)
  waiting for transfers between devices  1.85 us (1%)
  starting transfers between devices  1.51 us (1%)
    all_to_all x5, blocking collectives, exchange(): lax.all_to_all(blocks, AXES, 0, 0, tiled=True, axis_index_groups=groups)  99.6 us
    pallas_call x1, Pallas kernels, arrive_away(): pl.pallas_call(arrive_kernel, out_shape=(jax.ShapeDtypeStruct((64, 8, wid...  6.1 us
    pallas_call x1, Pallas kernels, spread_own(): pl.pallas_call(spread_kernel, out_shape=(shape, shape), in_specs=[SMEM] +...  3.01 us
    pallas_call x1, Pallas kernels, arrive_keep(): pl.pallas_call(keep_kernel, out_shape=jax.ShapeDtypeStruct((64, 8, width)...  2.99 us
  transfers between devices with their start and end apart: 4, of which 3 were waited for; matrix products, arithmetic and copies ran while one was open for 0% of the time, Pallas kernels for 6%

profile of v4, /device:TPU:0, one launch (start us, length us, event | category | flops | bytes accessed | tf_op | source)
XLA Modules:
  0.0 126.2 jit_solution(11795918787661889341)
XLA Ops:
  0.7 1.9 %dynamic-slice_bitcast_fusion = bf16[2,4,64,2048]{3,2,1,0:T(8,128)(2,1)S(1)} fusion(bf16[2,4,2,64,2048]{4,3,2,1,0:T(8,128)(2,1)} %bitcast.17, s32[]{:T(128)S(6)} %select_n.4), kind=kLoop, calls=%fused_computation.1 | loop fusion | bytes 4194308 | tf_op jit(solution)/shard_map/jit(dynamic_index_in_dim)/squeeze | solution.py:361
  2.6 0.5 collective-permute-start
  3.1 0.3 copy-done.3
  3.5 1.0 copy-done.4
  4.5 0.9 copy-done.6
  5.4 1.1 own_product.1.keep
  6.8 1.4 %both_products.1 = bf16[64,8,2048]{2,1,0:T(8,128)(2,1)S(1)} custom-call(s32[1,2]{1,0:T(1,128)S(1)} %collective-permute-done.peer, f32[32,1024]{1,0:T(8,128)S(1)} %copy-done.7, f32[2,4,2,64,32]{4,3,2,1,0:T(8,128)S(1)} %copy-done.4, bf16[2,4,64,2048]{3,2,1,0:T(8,128)(2,1)S(1)} %collective-permute-done.1.got, bf16[64,8,2048]{2,1,0:T(8,128)(2,1)S(1)} %own_product.1.keep), custom_call_target="tpu_custom_call" | custom-call | tf_op jit(solution)/shard_map/both_products/pallas_call | solution.py:166
  8.2 21.5 %all_to_all.25 = bf16[8,64,2048]{2,1,0:T(8,128)(2,1)S(1)} all-to-all(bf16[8,64,2048]{2,1,0:T(8,128)(2,1)S(1)} %bitcast.21), channel_id=1, replica_groups={{0,16,1,17,2,18,3,19},{48,32,49,33,50,34,51,35},{65,81,64,80,67,83,66,8..., dimensions={0} | all-to-all | bytes 4194304 | tf_op jit(solution)/shard_map/all_to_all | solution.py:298
  29.7 0.3 fusion
  30.3 27.4 %all_to_all.26.near = bf16[8,64,2048]{2,1,0:T(8,128)(2,1)S(1)} all-to-all(bf16[8,64,2048]{2,1,0:T(8,128)(2,1)S(1)} %broadcast_in_dim.9), channel_id=1, replica_groups={{0,48,65,113,6,54,71,119},{16,32,81,97,22,38,87,103},{1,49,64,112,7,55,..., dimensions={0} | all-to-all | bytes 4194304 | tf_op jit(solution)/shard_map/all_to_all | solution.py:298
  57.7 1.3 %mask_rows.1 = (bf16[8,64,2048]{2,1,0:T(8,128)(2,1)S(1)}, f32[8,2048]{1,0:T(8,128)}) custom-call(bf16[8,64,2048]{2,1,0:T(8,128)(2,1)S(1)} %all_to_all.26.near), custom_call_target="tpu_custom_call" | custom-call | tf_op jit(solution)/shard_map/mask_rows/pallas_call | solution.py:338
  59.0 19.1 %all_to_all.27 = bf16[8,64,2048]{2,1,0:T(8,128)(2,1)S(1)} all-to-all(bf16[8,64,2048]{2,1,0:T(8,128)(2,1)S(1)} %get-tuple-element.10), channel_id=1, replica_groups={{0,16,1,17,2,18,3,19},{48,32,49,33,50,34,51,35},{65,81,64,80,67,83,66,8..., dimensions={0} | all-to-all | bytes 4194304 | tf_op jit(solution)/shard_map/all_to_all | solution.py:298
  78.1 0.3 collective-permute-start.2
  78.5 3.0 %spread_own.1 = (bf16[2,4,1,64,1024]{4,3,2,1,0:T(8,128)(2,1)S(1)}, bf16[2,4,1,64,1024]{4,3,2,1,0:T(8,128)(2,1)S(1)}) custom-call(s32[1,2]{1,0:T(1,128)S(1)} %copy-done.8, f32[32,1024]{1,0:T(8,128)S(1)} %copy-done.7, f32[2,4,2,64,32]{4,3,2,1,0:T(8,128)S(1)} %copy-done.4, bf16[64,8,2048]{2,1,0:T(8,128)(2,1)S(1)} %bitcast.20, ...), custom_call_target="tpu_custom_call" | custom-call | tf_op jit(solution)/shard_map/spread_own/pallas_call | solution.py:236
  81.5 0.8 collective-permute-done.2.mask
  82.3 6.1 %arrive_away.1 = (bf16[64,8,2048]{2,1,0:T(8,128)(2,1)S(1)}, bf16[2,4,2,64,1024]{4,3,2,1,0:T(8,128)(2,1)S(1)}, bf16[2,4,2,64,1024]{4,3,2,1,0:T(8,128)(2,1)S(1)}) custom-call(s32[1,2]{1,0:T(1,128)S(1)} %copy-done.8, f32[32,1024]{1,0:T(8,128)S(1)} %copy-done.7, f32[2,4,2,64,32]{4,3,2,1,0:T(8,128)S(1)} %copy-done.5, ...), custom_call_target="tpu_custom_call" | custom-call | tf_op jit(solution)/shard_map/arrive_away/pallas_call | solution.py:265
  88.4 0.6 collective-permute-start.3
  89.0 3.0 %arrive_keep.1 = bf16[64,8,2048]{2,1,0:T(8,128)(2,1)S(1)} custom-call(bf16[2,4,2,64,1024]{4,3,2,1,0:T(8,128)(2,1)S(1)} %copy-done.1, bf16[2,4,2,64,1024]{4,3,2,1,0:T(8,128)(2,1)S(1)} %copy-done, bf16[2,4,2,64,1024]{4,3,2,1,0:T(8,128)(2,1)S(1)} %get-tuple-element.13.sums, bf16[2,4,2,64,1024]{4,3,2,1,0:T(8,128)(2,1)S(1)} %get-tuple-element.14.diffs, ...), custom_call_target="tpu_custom_call" | custom-call | tf_op jit(solution)/shard_map/arrive_keep/pallas_call | solution.py:286
  92.0 0.8 collective-permute-done.3
  92.8 0.8 add_convert_fusion
  93.6 18.9 %all_to_all.28 = bf16[8,64,2048]{2,1,0:T(8,128)(2,1)S(1)} all-to-all(bf16[8,64,2048]{2,1,0:T(8,128)(2,1)S(1)} %bitcast.22), channel_id=1, replica_groups={{0,16,1,17,2,18,3,19},{48,32,49,33,50,34,51,35},{65,81,64,80,67,83,66,8..., dimensions={0} | all-to-all | bytes 4194304 | tf_op jit(solution)/shard_map/all_to_all | solution.py:298
  112.5 0.3 fusion.1
  112.8 12.7 %all_to_all.29 = bf16[8,8,2048]{2,1,0:T(8,128)(2,1)S(1)} all-to-all(bf16[8,8,2048]{2,1,0:T(8,128)(2,1)S(1)} %fusion.1), channel_id=1, replica_groups={{0,48,65,113,6,54,71,119},{16,32,81,97,22,38,87,103},{1,49,64,112,7,55,..., dimensions={0} | all-to-all | bytes 524288 | tf_op jit(solution)/shard_map/all_to_all | solution.py:298
  125.6 0.7 maximum_divide_fusion
  (21 shorter events, 0.6 us)
Async XLA Ops:
  0.6 2.0 %copy-start.8 = (s32[1,2]{1,0:T(1,128)S(1)}, s32[1,2]{1,0:T(1,128)}, u32[]{:S(2)}) copy-start(s32[1,2]{1,0:T(1,128)} %modes.5) | copy-start | bytes 28
  0.6 2.8 %copy-start.3 = (bf16[1,1024,2048]{2,1,0:T(8,128)(2,1)S(1)}, bf16[1,1024,2048]{2,1,0:T(8,128)(2,1)}, u32[]{:S(2)}) copy-start(bf16[1,1024,2048]{2,1,0:T(8,128)(2,1)} %param.10) | copy-start | bytes 12582916
  2.5 4.2 %collective-permute-start.1 = (bf16[2,4,64,2048]{3,2,1,0:T(8,128)(2,1)S(1)}, bf16[2,4,64,2048]{3,2,1,0:T(8,128)(2,1)S(1)}, u32[]{:S(2)}, u32[]{:S(2)}) collective-permute-start(bf16[2,4,64,2048]{3,2,1,0:T(8,128)(2,1)S(1)} %dynamic-slice_bitcast_fusion), channel_id=1, source_target_pairs={{0,8},{8,0},{1,9},{9,1},{2,10},{10,2},{3,11},{11,3},{4,12},{12,4},... | collective-permute-start | bytes 6291464 | tf_op jit(solution)/shard_map/ppermute | solution.py:71
  2.6 4.1 %collective-permute-start = (s32[1,2]{1,0:T(1,128)S(1)}, s32[1,2]{1,0:T(1,128)S(1)}, u32[]{:S(2)}, u32[]{:S(2)}) collective-permute-start(s32[1,2]{1,0:T(1,128)S(1)} %copy-done.8), channel_id=1, source_target_pairs={{0,8},{8,0},{1,9},{9,1},{2,10},{10,2},{3,11},{11,3},{4,12},{12,4},... | collective-permute-start | bytes 32 | tf_op jit(solution)/shard_map/ppermute | solution.py:71
  3.5 1.0 copy-start.4
  4.5 0.9 copy-start.6
  5.4 1.4 %copy-start.7 = (f32[32,1024]{1,0:T(8,128)S(1)}, f32[32,1024]{1,0:T(8,128)}, u32[]{:S(2)}) copy-start(f32[32,1024]{1,0:T(8,128)} %constant.31.clone.table) | copy-start | bytes 393220
  59.0 19.5 %copy-start = (bf16[2,4,2,64,1024]{4,3,2,1,0:T(8,128)(2,1)S(1)}, bf16[2,4,2,64,1024]{4,3,2,1,0:T(8,128)(2,1)}, u32[]{:S(2)}) copy-start(bf16[2,4,2,64,1024]{4,3,2,1,0:T(8,128)(2,1)} %constant.50.odd) | copy-start | bytes 6291460
  59.0 19.5 %copy-start.1 = (bf16[2,4,2,64,1024]{4,3,2,1,0:T(8,128)(2,1)S(1)}, bf16[2,4,2,64,1024]{4,3,2,1,0:T(8,128)(2,1)}, u32[]{:S(2)}) copy-start(bf16[2,4,2,64,1024]{4,3,2,1,0:T(8,128)(2,1)} %constant.45.even) | copy-start | bytes 6291460
  78.1 4.2 %copy-start.2 = (bf16[1,1024,2048]{2,1,0:T(8,128)(2,1)S(1)}, bf16[1,1024,2048]{2,1,0:T(8,128)(2,1)}, u32[]{:S(2)}) copy-start(bf16[1,1024,2048]{2,1,0:T(8,128)(2,1)} %param.11) | copy-start | bytes 12582916
  78.1 4.2 %copy-start.5 = (f32[2,4,2,64,32]{4,3,2,1,0:T(8,128)S(1)}, f32[2,4,2,64,32]{4,3,2,1,0:T(8,128)}, u32[]{:S(2)}) copy-start(f32[2,4,2,64,32]{4,3,2,1,0:T(8,128)} %constant.40.columns) | copy-start | bytes 393220
  78.1 4.2 %collective-permute-start.2 = (bf16[64,8,2048]{2,1,0:T(8,128)(2,1)S(1)}, bf16[64,8,2048]{2,1,0:T(8,128)(2,1)S(1)}, u32[]{:S(2)}, u32[]{:S(2)}) collective-permute-start(bf16[64,8,2048]{2,1,0:T(8,128)(2,1)S(1)} %bitcast.19), channel_id=1, source_target_pairs={{0,8},{8,0},{1,9},{9,1},{2,10},{10,2},{3,11},{11,3},{4,12},{12,4},... | collective-permute-start | bytes 6291464 | tf_op jit(solution)/shard_map/ppermute | solution.py:71
  88.4 4.4 %collective-permute-start.3 = (bf16[64,8,2048]{2,1,0:T(8,128)(2,1)S(1)}, bf16[64,8,2048]{2,1,0:T(8,128)(2,1)S(1)}, u32[]{:S(2)}, u32[]{:S(2)}) collective-permute-start(bf16[64,8,2048]{2,1,0:T(8,128)(2,1)S(1)} %get-tuple-element.15), channel_id=1, source_target_pairs={{0,8},{8,0},{1,9},{9,1},{2,10},{10,2},{3,11},{11,3},{4,12},{12,4},... | collective-permute-start | bytes 6291464 | tf_op jit(solution)/shard_map/ppermute | solution.py:71

commit v5 on v4

--- a/solution.py
+++ b/solution.py
@@ -200,13 +200,15 @@
             diffs[plane, :, slot, :, where] = (top - bottom).reshape(4, 64, 256)
 
 
-def second_half(even, odd, sums, diffs, back, out, core):
+def second_half(even, odd, sums, diffs, back, out, core, chunks):
     cells = sums.shape[-1]
+    wide = out.shape[-1] // 2
     rows_even = even[:, :, core].reshape(512, cells)
     rows_odd = odd[:, :, core].reshape(512, cells)
-    for n in range(4):
+    for n in chunks:
         span = slice(n * 256, (n + 1) * 256)
         other = slice(cells + n * 256, cells + (n + 1) * 256)
+        at = (n - chunks[0]) * 256
         right_even = sums[:, :, :, :, span].reshape(cells, 256)
         right_odd = diffs[:, :, :, :, span].reshape(cells, 256)
         e, o = (
@@ -215,14 +217,15 @@
         )
         for j in range(32):
             for h in range(2):
-                at = slice(j * 8, j * 8 + 8)
-                real = e[0][at] - o[0][at] if h else e[0][at] + o[0][at]
-                imag = e[1][at] - o[1][at] if h else e[1][at] + o[1][at]
-                back_real = back[h, j // 8, j % 8 * 8 : j % 8 * 8 + 8, span].astype(F32)
-                back_imag = back[h, j // 8, j % 8 * 8 : j % 8 * 8 + 8, other].astype(F32)
+                rows = slice(j * 8, j * 8 + 8)
+                real = e[0][rows] - o[0][rows] if h else e[0][rows] + o[0][rows]
+                imag = e[1][rows] - o[1][rows] if h else e[1][rows] + o[1][rows]
+                inner = slice(j % 8 * 8, j % 8 * 8 + 8)
+                back_real = back[h, j // 8, core, inner, span].astype(F32)
+                back_imag = back[h, j // 8, core, inner, other].astype(F32)
                 place = place_of(h * 32 + j, core)
-                out[place, :, span] = (back_real * real + back_imag * imag).astype(BF16)
-                out[place, :, other] = (back_imag * real - back_real * imag).astype(BF16)
+                out[place, :, at : at + 256] = (back_real * real + back_imag * imag).astype(BF16)
+                out[place, :, wide + at : wide + at + 256] = (back_imag * real - back_real * imag).astype(BF16)
 
 
 def spread_kernel(modes, table, columns, mask, even, odd, sums, diffs, plus, minus):
@@ -244,54 +247,67 @@
     )(modes, table, columns, mask, even, odd)
 
 
-def arrive_kernel(
-    modes, table, columns, mask, even, odd, own_sums, own_diffs, back, out, sums, diffs, buf, plus, minus, sem
-):
+def arrive_kernel(modes, table, columns, mask, even, odd, own_sums, own_diffs, back, out, sums, diffs, plus, minus):
     core = lax.axis_index("core")
     other = 1 - core
-    copy = pltpu.make_async_copy(back.at[:, :, other], buf, sem)
-    copy.start()
     spread_half(modes, table, columns, mask, even, odd, plus, minus, sums, diffs, other, other)
     sums[:, :, core] = own_sums[:, :, 0]
     diffs[:, :, core] = own_diffs[:, :, 0]
-    copy.wait()
-    second_half(even, odd, sums, diffs, buf, out, other)
+    second_half(even, odd, sums, diffs, back, out, other, (0, 1))
 
 
 def arrive_away(modes, table, columns, mask, even, odd, own_sums, own_diffs, back):
-    width = back.shape[-1]
-    cells = width // 2
+    cells = back.shape[-1] // 2
     shape = jax.ShapeDtypeStruct((2, 4, 2, 64, cells), BF16)
     return pl.pallas_call(
         arrive_kernel,
-        out_shape=(jax.ShapeDtypeStruct((64, 8, width), BF16), shape, shape),
-        in_specs=[SMEM] + [VMEM] * 7 + [ANY],
+        out_shape=(jax.ShapeDtypeStruct((64, 8, cells), BF16), shape, shape),
+        in_specs=[SMEM] + [VMEM] * 8,
         out_specs=(VMEM, VMEM, VMEM),
-        scratch_shapes=[pltpu.VMEM((2, 4, 64, width), BF16)] + [pltpu.VMEM((512, cells), BF16)] * 2 + [DMA],
-        compiler_params=params(28),
+        scratch_shapes=[pltpu.VMEM((512, cells), BF16)] * 2,
+        compiler_params=params(32),
         name="arrive_away",
     )(modes, table, columns, mask, even, odd, own_sums, own_diffs, back)
 
 
-def keep_kernel(even, odd, sums, diffs, back, out, buf, sem):
+def rest_kernel(away, even, odd, sums, diffs, back, out):
     core = lax.axis_index("core")
-    copy = pltpu.make_async_copy(back.at[:, :, core], buf, sem)
-    copy.start()
-    copy.wait()
-    second_half(even, odd, sums, diffs, buf, out, core)
-
-
-def arrive_keep(even, odd, sums, diffs, back):
+    if away:
+        core = 1 - core
+    second_half(even, odd, sums, diffs, back, out, core, (2, 3) if away else (0, 1, 2, 3))
+
+
+def arrive_rest(away, even, odd, sums, diffs, back):
     width = back.shape[-1]
     return pl.pallas_call(
-        keep_kernel,
-        out_shape=jax.ShapeDtypeStruct((64, 8, width), BF16),
-        in_specs=[VMEM] * 4 + [ANY],
+        functools.partial(rest_kernel, away),
+        out_shape=jax.ShapeDtypeStruct((64, 8, width // 2 if away else width), BF16),
+        in_specs=[VMEM] * 5,
         out_specs=VMEM,
-        scratch_shapes=[pltpu.VMEM((2, 4, 64, width), BF16), DMA],
-        compiler_params=params(20),
-        name="arrive_keep",
+        compiler_params=params(22),
+        cost_estimate=pl.CostEstimate(flops=(2 << 30) >> away, bytes_accessed=8 << 20, transcendentals=0),
+        name="arrive_rest" if away else "arrive_keep",
     )(even, odd, sums, diffs, back)
+
+
+def join_kernel(keep, first, second, out):
+    half = first.shape[-1] // 2
+    for place in range(64):
+        for n in range(4):
+            part = (first, second)[n % 2][place, :, (n // 2) * half : (n // 2 + 1) * half]
+            span = slice(n * half, (n + 1) * half)
+            out[place, :, span] = (keep[place, :, span].astype(F32) + part.astype(F32)).astype(BF16)
+
+
+def join(keep, first, second):
+    return pl.pallas_call(
+        join_kernel,
+        out_shape=jax.ShapeDtypeStruct(keep.shape, BF16),
+        in_specs=[VMEM] * 3,
+        out_specs=VMEM,
+        compiler_params=params(14),
+        name="join",
+    )(keep, first, second)
 
 
 def exchange(blocks, groups):
@@ -369,9 +385,10 @@
     other = swap_cores(mine)
     own = spread_own(modes, table, columns, mine, even, odd)
     away, sums, diffs = arrive_away(modes, table, columns, other, even, odd, *own, back_second)
-    got = swap_cores(away)
-    keep = arrive_keep(even, odd, sums, diffs, back_second)
-    partial = halve_rows((keep.astype(F32) + got.astype(F32)).astype(BF16))
+    first = swap_cores(away)
+    second = swap_cores(arrive_rest(True, even, odd, sums, diffs, back_second))
+    keep = arrive_rest(False, even, odd, sums, diffs, back_second)
+    partial = halve_rows(join(keep, first, second))
     parts = exchange(partial.reshape(8, 8, width), NARROW)
     mask_second = soften(total(parts) * scale_all)
     return (mask_first, mask_second)

time: 127 us -> 126 us (level)
    pallas_call x2 -> x4, Pallas kernels: 9.09 us -> 9.41 us  [the longest x1 4.48 us: arrive_away(): pl.pallas_call(arrive_kernel, out_shape=(jax.ShapeDtypeStruct((64, 8, cel...]
  transfers between devices with their start and end apart: 4 -> 5, of which waited for: 3 -> 3; matrix products, arithmetic and copies ran while one was open for 0% -> 0% of each run, Pallas kernels for 6% -> 6%
where the time goes in v5:
time: 126 us
  blocking collectives  99.6 us (79%)
  Pallas kernels  16.3 us (13%)
  local copies, waits for them, and re-layouts  4.43 us (4%)
  waiting for transfers between devices  1.66 us (1%)
  starting transfers between devices  1.59 us (1%)
  other arithmetic  1.39 us (1%)
    all_to_all x5, blocking collectives, exchange(): lax.all_to_all(blocks, AXES, 0, 0, tiled=True, axis_index_groups=groups)  99.6 us
    pallas_call x1, Pallas kernels, arrive_away(): pl.pallas_call(arrive_kernel, out_shape=(jax.ShapeDtypeStruct((64, 8, cel...  4.48 us
    pallas_call x2, Pallas kernels, arrive_rest(): pl.pallas_call(functools.partial(rest_kernel, away), out_shape=jax.ShapeD...  4.45 us
    pallas_call x1, Pallas kernels, spread_own(): pl.pallas_call(spread_kernel, out_shape=(shape, shape), in_specs=[SMEM] +...  3.01 us
  transfers between devices with their start and end apart: 5, of which 3 were waited for; matrix products, arithmetic and copies ran while one was open for 0% of the time, Pallas kernels for 6%

profile of v5, /device:TPU:0, one launch (start us, length us, event | category | flops | bytes accessed | tf_op | source)
XLA Modules:
  0.0 125.7 jit_solution(3150132198433342168)
XLA Ops:
  0.7 1.9 %dynamic-slice_bitcast_fusion = bf16[2,4,64,2048]{3,2,1,0:T(8,128)(2,1)S(1)} fusion(bf16[2,4,2,64,2048]{4,3,2,1,0:T(8,128)(2,1)} %bitcast.18, s32[]{:T(128)S(6)} %select_n.4), kind=kLoop, calls=%fused_computation | loop fusion | bytes 4194308 | tf_op jit(solution)/shard_map/jit(dynamic_index_in_dim)/squeeze | solution.py:377
  2.6 0.5 collective-permute-start
  3.1 0.3 copy-done.3
  3.5 1.0 copy-done.4
  4.5 0.9 copy-done.6
  5.4 1.1 own_product.1.keep
  6.8 1.4 %both_products.1 = bf16[64,8,2048]{2,1,0:T(8,128)(2,1)S(1)} custom-call(s32[1,2]{1,0:T(1,128)S(1)} %collective-permute-done.peer, f32[32,1024]{1,0:T(8,128)S(1)} %copy-done.7, f32[2,4,2,64,32]{4,3,2,1,0:T(8,128)S(1)} %copy-done.4, bf16[2,4,64,2048]{3,2,1,0:T(8,128)(2,1)S(1)} %collective-permute-done.1.got, bf16[64,8,2048]{2,1,0:T(8,128)(2,1)S(1)} %own_product.1.keep), custom_call_target="tpu_custom_call" | custom-call | tf_op jit(solution)/shard_map/both_products/pallas_call | solution.py:166
  8.2 21.5 %all_to_all.25 = bf16[8,64,2048]{2,1,0:T(8,128)(2,1)S(1)} all-to-all(bf16[8,64,2048]{2,1,0:T(8,128)(2,1)S(1)} %bitcast.23), channel_id=1, replica_groups={{0,16,1,17,2,18,3,19},{48,32,49,33,50,34,51,35},{65,81,64,80,67,83,66,8..., dimensions={0} | all-to-all | bytes 4194304 | tf_op jit(solution)/shard_map/all_to_all | solution.py:314
  30.3 27.4 %all_to_all.26.near = bf16[8,64,2048]{2,1,0:T(8,128)(2,1)S(1)} all-to-all(bf16[8,64,2048]{2,1,0:T(8,128)(2,1)S(1)} %broadcast_in_dim.9), channel_id=1, replica_groups={{0,48,65,113,6,54,71,119},{16,32,81,97,22,38,87,103},{1,49,64,112,7,55,..., dimensions={0} | all-to-all | bytes 4194304 | tf_op jit(solution)/shard_map/all_to_all | solution.py:314
  57.7 1.3 %mask_rows.1 = (bf16[8,64,2048]{2,1,0:T(8,128)(2,1)S(1)}, f32[8,2048]{1,0:T(8,128)}) custom-call(bf16[8,64,2048]{2,1,0:T(8,128)(2,1)S(1)} %all_to_all.26.near), custom_call_target="tpu_custom_call" | custom-call | tf_op jit(solution)/shard_map/mask_rows/pallas_call | solution.py:354
  59.0 19.1 %all_to_all.27 = bf16[8,64,2048]{2,1,0:T(8,128)(2,1)S(1)} all-to-all(bf16[8,64,2048]{2,1,0:T(8,128)(2,1)S(1)} %get-tuple-element.10), channel_id=1, replica_groups={{0,16,1,17,2,18,3,19},{48,32,49,33,50,34,51,35},{65,81,64,80,67,83,66,8..., dimensions={0} | all-to-all | bytes 4194304 | tf_op jit(solution)/shard_map/all_to_all | solution.py:314
  78.1 0.3 collective-permute-start.2
  78.5 3.0 %spread_own.1 = (bf16[2,4,1,64,1024]{4,3,2,1,0:T(8,128)(2,1)S(1)}, bf16[2,4,1,64,1024]{4,3,2,1,0:T(8,128)(2,1)S(1)}) custom-call(s32[1,2]{1,0:T(1,128)S(1)} %copy-done.8, f32[32,1024]{1,0:T(8,128)S(1)} %copy-done.7, f32[2,4,2,64,32]{4,3,2,1,0:T(8,128)S(1)} %copy-done.4, bf16[64,8,2048]{2,1,0:T(8,128)(2,1)S(1)} %bitcast.22, ...), custom_call_target="tpu_custom_call" | custom-call | tf_op jit(solution)/shard_map/spread_own/pallas_call | solution.py:239
  81.5 0.8 collective-permute-done.2.mask
  82.3 4.5 %arrive_away.1 = (bf16[64,8,1024]{2,1,0:T(8,128)(2,1)S(1)}, bf16[2,4,2,64,1024]{4,3,2,1,0:T(8,128)(2,1)S(1)}, bf16[2,4,2,64,1024]{4,3,2,1,0:T(8,128)(2,1)S(1)}) custom-call(s32[1,2]{1,0:T(1,128)S(1)} %copy-done.8, f32[32,1024]{1,0:T(8,128)S(1)} %copy-done.7, f32[2,4,2,64,32]{4,3,2,1,0:T(8,128)S(1)} %copy-done.5, ...), custom_call_target="tpu_custom_call" | custom-call | tf_op jit(solution)/shard_map/arrive_away/pallas_call | solution.py:262
  86.8 1.5 %arrive_rest.1 = bf16[64,8,1024]{2,1,0:T(8,128)(2,1)S(1)} custom-call(bf16[2,4,2,64,1024]{4,3,2,1,0:T(8,128)(2,1)S(1)} %copy-done.2, bf16[2,4,2,64,1024]{4,3,2,1,0:T(8,128)(2,1)S(1)} %copy-done.1, bf16[2,4,2,64,1024]{4,3,2,1,0:T(8,128)(2,1)S(1)} %get-tuple-element.13.sums, bf16[2,4,2,64,1024]{4,3,2,1,0:T(8,128)(2,1)S(1)} %get-tuple-element.14.diffs, ...), custom_call_target="tpu_custom_call" | custom-call | flops 1073741824 | bytes 8388608 | tf_op jit(solution)/shard_map/arrive_rest/pallas_call | solution.py:282
  88.3 0.4 collective-permute-start.4
  89.0 2.9 %arrive_keep.1.keep = bf16[64,8,2048]{2,1,0:T(8,128)(2,1)S(1)} custom-call(bf16[2,4,2,64,1024]{4,3,2,1,0:T(8,128)(2,1)S(1)} %copy-done.2, bf16[2,4,2,64,1024]{4,3,2,1,0:T(8,128)(2,1)S(1)} %copy-done.1, bf16[2,4,2,64,1024]{4,3,2,1,0:T(8,128)(2,1)S(1)} %get-tuple-element.13.sums, bf16[2,4,2,64,1024]{4,3,2,1,0:T(8,128)(2,1)S(1)} %get-tuple-element.14.diffs, ...), custom_call_target="tpu_custom_call" | custom-call | flops 2147483648 | bytes 8388608 | tf_op jit(solution)/shard_map/arrive_keep/pallas_call | solution.py:282
  91.9 0.6 collective-permute-done.3.first
  92.6 0.5 join.1
  93.0 18.9 %all_to_all.28 = bf16[8,64,2048]{2,1,0:T(8,128)(2,1)S(1)} all-to-all(bf16[8,64,2048]{2,1,0:T(8,128)(2,1)S(1)} %bitcast.20), channel_id=1, replica_groups={{0,16,1,17,2,18,3,19},{48,32,49,33,50,34,51,35},{65,81,64,80,67,83,66,8..., dimensions={0} | all-to-all | bytes 4194304 | tf_op jit(solution)/shard_map/all_to_all | solution.py:314
  111.9 0.3 fusion.1
  112.3 12.7 %all_to_all.29 = bf16[8,8,2048]{2,1,0:T(8,128)(2,1)S(1)} all-to-all(bf16[8,8,2048]{2,1,0:T(8,128)(2,1)S(1)} %fusion.1), channel_id=1, replica_groups={{0,48,65,113,6,54,71,119},{16,32,81,97,22,38,87,103},{1,49,64,112,7,55,..., dimensions={0} | all-to-all | bytes 524288 | tf_op jit(solution)/shard_map/all_to_all | solution.py:314
  125.0 0.7 maximum_divide_fusion
  (24 shorter events, 1.2 us)
Async XLA Ops:
  0.6 2.0 %copy-start.8 = (s32[1,2]{1,0:T(1,128)S(1)}, s32[1,2]{1,0:T(1,128)}, u32[]{:S(2)}) copy-start(s32[1,2]{1,0:T(1,128)} %modes.5) | copy-start | bytes 28
  0.6 2.8 %copy-start.3 = (bf16[1,1024,2048]{2,1,0:T(8,128)(2,1)S(1)}, bf16[1,1024,2048]{2,1,0:T(8,128)(2,1)}, u32[]{:S(2)}) copy-start(bf16[1,1024,2048]{2,1,0:T(8,128)(2,1)} %param.10) | copy-start | bytes 12582916
  2.5 4.2 %collective-permute-start.1 = (bf16[2,4,64,2048]{3,2,1,0:T(8,128)(2,1)S(1)}, bf16[2,4,64,2048]{3,2,1,0:T(8,128)(2,1)S(1)}, u32[]{:S(2)}, u32[]{:S(2)}) collective-permute-start(bf16[2,4,64,2048]{3,2,1,0:T(8,128)(2,1)S(1)} %dynamic-slice_bitcast_fusion), channel_id=1, source_target_pairs={{0,8},{8,0},{1,9},{9,1},{2,10},{10,2},{3,11},{11,3},{4,12},{12,4},... | collective-permute-start | bytes 6291464 | tf_op jit(solution)/shard_map/ppermute | solution.py:71
  2.6 4.1 %collective-permute-start = (s32[1,2]{1,0:T(1,128)S(1)}, s32[1,2]{1,0:T(1,128)S(1)}, u32[]{:S(2)}, u32[]{:S(2)}) collective-permute-start(s32[1,2]{1,0:T(1,128)S(1)} %copy-done.8), channel_id=1, source_target_pairs={{0,8},{8,0},{1,9},{9,1},{2,10},{10,2},{3,11},{11,3},{4,12},{12,4},... | collective-permute-start | bytes 32 | tf_op jit(solution)/shard_map/ppermute | solution.py:71
  3.5 1.0 copy-start.4
  4.5 0.9 copy-start.6
  5.4 1.4 %copy-start.7 = (f32[32,1024]{1,0:T(8,128)S(1)}, f32[32,1024]{1,0:T(8,128)}, u32[]{:S(2)}) copy-start(f32[32,1024]{1,0:T(8,128)} %constant.31.clone.table) | copy-start | bytes 393220
  59.0 19.5 %copy-start.1 = (bf16[2,4,2,64,1024]{4,3,2,1,0:T(8,128)(2,1)S(1)}, bf16[2,4,2,64,1024]{4,3,2,1,0:T(8,128)(2,1)}, u32[]{:S(2)}) copy-start(bf16[2,4,2,64,1024]{4,3,2,1,0:T(8,128)(2,1)} %constant.50.odd) | copy-start | bytes 6291460
  59.0 19.5 %copy-start.2 = (bf16[2,4,2,64,1024]{4,3,2,1,0:T(8,128)(2,1)S(1)}, bf16[2,4,2,64,1024]{4,3,2,1,0:T(8,128)(2,1)}, u32[]{:S(2)}) copy-start(bf16[2,4,2,64,1024]{4,3,2,1,0:T(8,128)(2,1)} %constant.45.even) | copy-start | bytes 6291460
  78.1 4.2 %copy-start = (bf16[1,1024,2048]{2,1,0:T(8,128)(2,1)S(1)}, bf16[1,1024,2048]{2,1,0:T(8,128)(2,1)}, u32[]{:S(2)}) copy-start(bf16[1,1024,2048]{2,1,0:T(8,128)(2,1)} %param.11) | copy-start | bytes 12582916
  78.1 4.2 %copy-start.5 = (f32[2,4,2,64,32]{4,3,2,1,0:T(8,128)S(1)}, f32[2,4,2,64,32]{4,3,2,1,0:T(8,128)}, u32[]{:S(2)}) copy-start(f32[2,4,2,64,32]{4,3,2,1,0:T(8,128)} %constant.40.columns) | copy-start | bytes 393220
  78.1 4.2 %collective-permute-start.2 = (bf16[64,8,2048]{2,1,0:T(8,128)(2,1)S(1)}, bf16[64,8,2048]{2,1,0:T(8,128)(2,1)S(1)}, u32[]{:S(2)}, u32[]{:S(2)}) collective-permute-start(bf16[64,8,2048]{2,1,0:T(8,128)(2,1)S(1)} %bitcast.21), channel_id=1, source_target_pairs={{0,8},{8,0},{1,9},{9,1},{2,10},{10,2},{3,11},{11,3},{4,12},{12,4},... | collective-permute-start | bytes 6291464 | tf_op jit(solution)/shard_map/ppermute | solution.py:71
  88.3 3.6 %collective-permute-start.4 = (bf16[64,8,1024]{2,1,0:T(8,128)(2,1)S(1)}, bf16[64,8,1024]{2,1,0:T(8,128)(2,1)S(1)}, u32[]{:S(2)}, u32[]{:S(2)}) collective-permute-start(bf16[64,8,1024]{2,1,0:T(8,128)(2,1)S(1)} %arrive_rest.1), channel_id=1, source_target_pairs={{0,8},{8,0},{1,9},{9,1},{2,10},{10,2},{3,11},{11,3},{4,12},{12,4},... | collective-permute-start | bytes 3145736 | tf_op jit(solution)/shard_map/ppermute | solution.py:71
  88.7 3.8 %collective-permute-start.3 = (bf16[64,8,1024]{2,1,0:T(8,128)(2,1)S(1)}, bf16[64,8,1024]{2,1,0:T(8,128)(2,1)S(1)}, u32[]{:S(2)}, u32[]{:S(2)}) collective-permute-start(bf16[64,8,1024]{2,1,0:T(8,128)(2,1)S(1)} %get-tuple-element.15), channel_id=1, source_target_pairs={{0,8},{8,0},{1,9},{9,1},{2,10},{10,2},{3,11},{11,3},{4,12},{12,4},... | collective-permute-start | bytes 3145736 | tf_op jit(solution)/shard_map/ppermute | solution.py:71

commit v6 on v5

--- a/solution.py
+++ b/solution.py
@@ -155,11 +155,10 @@
     for block in range(64):
         place = place_of(block, core)
         k, j = block // 8, block % 8
-        field = (row_func[block * 8 : block * 8 + 8] * col_func).astype(BF16).astype(F32)
+        field = (row_func[block * 8 : block * 8 + 8] * col_func).astype(BF16)
         for plane in range(2):
             span = slice(plane * cells, (plane + 1) * cells)
-            value = got[k // 4, k % 4, j * 8 : j * 8 + 8, span].astype(F32) * field
-            out[place, :, span] = (value + keep[place, :, span].astype(F32)).astype(BF16)
+            out[place, :, span] = got[k // 4, k % 4, j * 8 : j * 8 + 8, span] * field + keep[place, :, span]
 
 
 def both_products(peer, table, columns, got, keep):
@@ -296,7 +295,7 @@
         for n in range(4):
             part = (first, second)[n % 2][place, :, (n // 2) * half : (n // 2 + 1) * half]
             span = slice(n * half, (n + 1) * half)
-            out[place, :, span] = (keep[place, :, span].astype(F32) + part.astype(F32)).astype(BF16)
+            out[place, :, span] = keep[place, :, span] + part
 
 
 def join(keep, first, second):
@@ -324,6 +323,27 @@
 def halve_rows(both):
     width = both.shape[-1]
     return total(exchange(both.reshape(8, 64, width), WIDE)).astype(BF16)
+
+
+def partial_kernel(wide, out):
+    half = wide.shape[-1] // 2
+    for block in range(8):
+        rows = slice(block * 8, block * 8 + 8)
+        for span in (slice(0, half), slice(half, 2 * half)):
+            part = total([wide[k, rows, span] for k in range(8)]).astype(BF16)
+            for k in range(8):
+                out[k, rows, span] = part
+
+
+def partial_rows(wide):
+    return pl.pallas_call(
+        partial_kernel,
+        out_shape=jax.ShapeDtypeStruct(wide.shape, BF16),
+        in_specs=[VMEM],
+        out_specs=VMEM,
+        compiler_params=params(12),
+        name="partial_rows",
+    )(wide)
 
 
 def own_place():
@@ -377,16 +397,17 @@
     away = lax.dynamic_index_in_dim(back_first, 1 - lax.axis_index("core"), 2, keepdims=False)
     got = swap_cores(away)
     keep = own_product(modes, table, columns, back_first)
-    partial = halve_rows(both_products(peer, table, columns, got, keep))
     width = 2 * cells
-    near = exchange(jnp.broadcast_to(partial[None], (8, 64, width)), NARROW)
+    both = both_products(peer, table, columns, got, keep)
+    near = exchange(partial_rows(exchange(both.reshape(8, 64, width), WIDE)), NARROW)
     low, mask_first = mask_rows(near, scale_all)
     mine = exchange(low, WIDE).reshape(64, 8, width)
     other = swap_cores(mine)
     own = spread_own(modes, table, columns, mine, even, odd)
     away, sums, diffs = arrive_away(modes, table, columns, other, even, odd, *own, back_second)
     first = swap_cores(away)
-    second = swap_cores(arrive_rest(True, even, odd, sums, diffs, back_second))
+    rest = arrive_rest(True, even, odd, sums, diffs, back_second)
+    second = swap_cores(rest)
     keep = arrive_rest(False, even, odd, sums, diffs, back_second)
     partial = halve_rows(join(keep, first, second))
     parts = exchange(partial.reshape(8, 8, width), NARROW)

time: 126 us -> 125 us (level)
  no operation moved by 1% of the time
where the time goes in v6:
time: 125 us
  blocking collectives  99.6 us (80%)
  Pallas kernels  15.8 us (13%)
  local copies, waits for them, and re-layouts  4.19 us (3%)
  waiting for transfers between devices  1.66 us (1%)
  starting transfers between devices  1.59 us (1%)
    all_to_all x5, blocking collectives, exchange(): lax.all_to_all(blocks, AXES, 0, 0, tiled=True, axis_index_groups=groups)  99.6 us
    pallas_call x1, Pallas kernels, arrive_away(): pl.pallas_call(arrive_kernel, out_shape=(jax.ShapeDtypeStruct((64, 8, cel...  4.48 us
    pallas_call x2, Pallas kernels, arrive_rest(): pl.pallas_call(functools.partial(rest_kernel, away), out_shape=jax.ShapeD...  4.45 us
    pallas_call x1, Pallas kernels, spread_own(): pl.pallas_call(spread_kernel, out_shape=(shape, shape), in_specs=[SMEM] +...  3.01 us
  transfers between devices with their start and end apart: 5, of which 3 were waited for; matrix products, arithmetic and copies ran while one was open for 0% of the time, Pallas kernels for 6%

profile of v6, /device:TPU:0, one launch (start us, length us, event | category | flops | bytes accessed | tf_op | source)
XLA Modules:
  0.0 124.6 jit_solution(2966804494402069774)
XLA Ops:
  0.7 1.9 %dynamic-slice_bitcast_fusion = bf16[2,4,64,2048]{3,2,1,0:T(8,128)(2,1)S(1)} fusion(bf16[2,4,2,64,2048]{4,3,2,1,0:T(8,128)(2,1)} %bitcast.16, s32[]{:T(128)S(6)} %select_n.4), kind=kLoop, calls=%fused_computation | loop fusion | bytes 4194308 | tf_op jit(solution)/shard_map/jit(dynamic_index_in_dim)/squeeze | solution.py:397
  2.6 0.5 collective-permute-start
  3.1 0.3 copy-done.3
  3.5 1.0 copy-done.4
  4.5 0.9 copy-done.6
  5.4 1.1 own_product.1.keep
  6.8 1.0 both_products.1
  7.8 21.5 %all_to_all.25.wide = bf16[8,64,2048]{2,1,0:T(8,128)(2,1)S(1)} all-to-all(bf16[8,64,2048]{2,1,0:T(8,128)(2,1)S(1)} %bitcast.21), channel_id=1, replica_groups={{0,16,1,17,2,18,3,19},{48,32,49,33,50,34,51,35},{65,81,64,80,67,83,66,8..., dimensions={0} | all-to-all | bytes 4194304 | tf_op jit(solution)/shard_map/all_to_all | solution.py:313
  29.6 27.4 %all_to_all.26.near = bf16[8,64,2048]{2,1,0:T(8,128)(2,1)S(1)} all-to-all(bf16[8,64,2048]{2,1,0:T(8,128)(2,1)S(1)} %partial_rows.1), channel_id=1, replica_groups={{0,48,65,113,6,54,71,119},{16,32,81,97,22,38,87,103},{1,49,64,112,7,55,..., dimensions={0} | all-to-all | bytes 4194304 | tf_op jit(solution)/shard_map/all_to_all | solution.py:313
  56.9 1.3 %mask_rows.1 = (bf16[8,64,2048]{2,1,0:T(8,128)(2,1)S(1)}, f32[8,2048]{1,0:T(8,128)}) custom-call(bf16[8,64,2048]{2,1,0:T(8,128)(2,1)S(1)} %all_to_all.26.near), custom_call_target="tpu_custom_call" | custom-call | tf_op jit(solution)/shard_map/mask_rows/pallas_call | solution.py:374
  58.2 19.1 %all_to_all.27 = bf16[8,64,2048]{2,1,0:T(8,128)(2,1)S(1)} all-to-all(bf16[8,64,2048]{2,1,0:T(8,128)(2,1)S(1)} %get-tuple-element.10), channel_id=1, replica_groups={{0,16,1,17,2,18,3,19},{48,32,49,33,50,34,51,35},{65,81,64,80,67,83,66,8..., dimensions={0} | all-to-all | bytes 4194304 | tf_op jit(solution)/shard_map/all_to_all | solution.py:313
  77.3 0.3 collective-permute-start.2
  77.7 3.0 %spread_own.1 = (bf16[2,4,1,64,1024]{4,3,2,1,0:T(8,128)(2,1)S(1)}, bf16[2,4,1,64,1024]{4,3,2,1,0:T(8,128)(2,1)S(1)}) custom-call(s32[1,2]{1,0:T(1,128)S(1)} %copy-done.8, f32[32,1024]{1,0:T(8,128)S(1)} %copy-done.7, f32[2,4,2,64,32]{4,3,2,1,0:T(8,128)S(1)} %copy-done.4, bf16[64,8,2048]{2,1,0:T(8,128)(2,1)S(1)} %bitcast.20, ...), custom_call_target="tpu_custom_call" | custom-call | tf_op jit(solution)/shard_map/spread_own/pallas_call | solution.py:238
  80.7 0.8 collective-permute-done.2.mask
  81.5 4.5 %arrive_away.1 = (bf16[64,8,1024]{2,1,0:T(8,128)(2,1)S(1)}, bf16[2,4,2,64,1024]{4,3,2,1,0:T(8,128)(2,1)S(1)}, bf16[2,4,2,64,1024]{4,3,2,1,0:T(8,128)(2,1)S(1)}) custom-call(s32[1,2]{1,0:T(1,128)S(1)} %copy-done.8, f32[32,1024]{1,0:T(8,128)S(1)} %copy-done.7, f32[2,4,2,64,32]{4,3,2,1,0:T(8,128)S(1)} %copy-done.5, ...), custom_call_target="tpu_custom_call" | custom-call | tf_op jit(solution)/shard_map/arrive_away/pallas_call | solution.py:261
  86.0 1.5 %arrive_rest.1 = bf16[64,8,1024]{2,1,0:T(8,128)(2,1)S(1)} custom-call(bf16[2,4,2,64,1024]{4,3,2,1,0:T(8,128)(2,1)S(1)} %copy-done.2, bf16[2,4,2,64,1024]{4,3,2,1,0:T(8,128)(2,1)S(1)} %copy-done.1, bf16[2,4,2,64,1024]{4,3,2,1,0:T(8,128)(2,1)S(1)} %get-tuple-element.13.sums, bf16[2,4,2,64,1024]{4,3,2,1,0:T(8,128)(2,1)S(1)} %get-tuple-element.14.diffs, ...), custom_call_target="tpu_custom_call" | custom-call | flops 1073741824 | bytes 8388608 | tf_op jit(solution)/shard_map/arrive_rest/pallas_call | solution.py:281
  87.5 0.4 collective-permute-start.4
  88.0 0.3 collective-permute-start.3
  88.2 2.9 %arrive_keep.1.keep = bf16[64,8,2048]{2,1,0:T(8,128)(2,1)S(1)} custom-call(bf16[2,4,2,64,1024]{4,3,2,1,0:T(8,128)(2,1)S(1)} %copy-done.2, bf16[2,4,2,64,1024]{4,3,2,1,0:T(8,128)(2,1)S(1)} %copy-done.1, bf16[2,4,2,64,1024]{4,3,2,1,0:T(8,128)(2,1)S(1)} %get-tuple-element.13.sums, bf16[2,4,2,64,1024]{4,3,2,1,0:T(8,128)(2,1)S(1)} %get-tuple-element.14.diffs, ...), custom_call_target="tpu_custom_call" | custom-call | flops 2147483648 | bytes 8388608 | tf_op jit(solution)/shard_map/arrive_keep/pallas_call | solution.py:281
  91.2 0.6 collective-permute-done.3.first
  92.0 18.9 %all_to_all.28 = bf16[8,64,2048]{2,1,0:T(8,128)(2,1)S(1)} all-to-all(bf16[8,64,2048]{2,1,0:T(8,128)(2,1)S(1)} %bitcast.18), channel_id=1, replica_groups={{0,16,1,17,2,18,3,19},{48,32,49,33,50,34,51,35},{65,81,64,80,67,83,66,8..., dimensions={0} | all-to-all | bytes 4194304 | tf_op jit(solution)/shard_map/all_to_all | solution.py:313
  110.9 0.3 fusion
  111.2 12.7 %all_to_all.29 = bf16[8,8,2048]{2,1,0:T(8,128)(2,1)S(1)} all-to-all(bf16[8,8,2048]{2,1,0:T(8,128)(2,1)S(1)} %fusion), channel_id=1, replica_groups={{0,48,65,113,6,54,71,119},{16,32,81,97,22,38,87,103},{1,49,64,112,7,55,..., dimensions={0} | all-to-all | bytes 524288 | tf_op jit(solution)/shard_map/all_to_all | solution.py:313
  124.0 0.7 maximum_divide_fusion
  (23 shorter events, 0.9 us)
Async XLA Ops:
  0.6 2.0 %copy-start.8 = (s32[1,2]{1,0:T(1,128)S(1)}, s32[1,2]{1,0:T(1,128)}, u32[]{:S(2)}) copy-start(s32[1,2]{1,0:T(1,128)} %modes.5) | copy-start | bytes 28
  0.6 2.8 %copy-start.3 = (bf16[1,1024,2048]{2,1,0:T(8,128)(2,1)S(1)}, bf16[1,1024,2048]{2,1,0:T(8,128)(2,1)}, u32[]{:S(2)}) copy-start(bf16[1,1024,2048]{2,1,0:T(8,128)(2,1)} %param.10) | copy-start | bytes 12582916
  2.5 4.2 %collective-permute-start.1 = (bf16[2,4,64,2048]{3,2,1,0:T(8,128)(2,1)S(1)}, bf16[2,4,64,2048]{3,2,1,0:T(8,128)(2,1)S(1)}, u32[]{:S(2)}, u32[]{:S(2)}) collective-permute-start(bf16[2,4,64,2048]{3,2,1,0:T(8,128)(2,1)S(1)} %dynamic-slice_bitcast_fusion), channel_id=1, source_target_pairs={{0,8},{8,0},{1,9},{9,1},{2,10},{10,2},{3,11},{11,3},{4,12},{12,4},... | collective-permute-start | bytes 6291464 | tf_op jit(solution)/shard_map/ppermute | solution.py:71
  2.6 4.1 %collective-permute-start = (s32[1,2]{1,0:T(1,128)S(1)}, s32[1,2]{1,0:T(1,128)S(1)}, u32[]{:S(2)}, u32[]{:S(2)}) collective-permute-start(s32[1,2]{1,0:T(1,128)S(1)} %copy-done.8), channel_id=1, source_target_pairs={{0,8},{8,0},{1,9},{9,1},{2,10},{10,2},{3,11},{11,3},{4,12},{12,4},... | collective-permute-start | bytes 32 | tf_op jit(solution)/shard_map/ppermute | solution.py:71
  3.5 1.0 copy-start.4
  4.5 0.9 copy-start.6
  5.4 1.4 %copy-start.7 = (f32[32,1024]{1,0:T(8,128)S(1)}, f32[32,1024]{1,0:T(8,128)}, u32[]{:S(2)}) copy-start(f32[32,1024]{1,0:T(8,128)} %constant.31.clone.table) | copy-start | bytes 393220
  58.2 19.5 %copy-start.1 = (bf16[2,4,2,64,1024]{4,3,2,1,0:T(8,128)(2,1)S(1)}, bf16[2,4,2,64,1024]{4,3,2,1,0:T(8,128)(2,1)}, u32[]{:S(2)}) copy-start(bf16[2,4,2,64,1024]{4,3,2,1,0:T(8,128)(2,1)} %constant.50.odd) | copy-start | bytes 6291460
  58.2 19.5 %copy-start.2 = (bf16[2,4,2,64,1024]{4,3,2,1,0:T(8,128)(2,1)S(1)}, bf16[2,4,2,64,1024]{4,3,2,1,0:T(8,128)(2,1)}, u32[]{:S(2)}) copy-start(bf16[2,4,2,64,1024]{4,3,2,1,0:T(8,128)(2,1)} %constant.45.even) | copy-start | bytes 6291460
  77.3 4.2 %copy-start = (bf16[1,1024,2048]{2,1,0:T(8,128)(2,1)S(1)}, bf16[1,1024,2048]{2,1,0:T(8,128)(2,1)}, u32[]{:S(2)}) copy-start(bf16[1,1024,2048]{2,1,0:T(8,128)(2,1)} %param.11) | copy-start | bytes 12582916
  77.3 4.2 %copy-start.5 = (f32[2,4,2,64,32]{4,3,2,1,0:T(8,128)S(1)}, f32[2,4,2,64,32]{4,3,2,1,0:T(8,128)}, u32[]{:S(2)}) copy-start(f32[2,4,2,64,32]{4,3,2,1,0:T(8,128)} %constant.40.columns) | copy-start | bytes 393220
  77.3 4.2 %collective-permute-start.2 = (bf16[64,8,2048]{2,1,0:T(8,128)(2,1)S(1)}, bf16[64,8,2048]{2,1,0:T(8,128)(2,1)S(1)}, u32[]{:S(2)}, u32[]{:S(2)}) collective-permute-start(bf16[64,8,2048]{2,1,0:T(8,128)(2,1)S(1)} %bitcast.19), channel_id=1, source_target_pairs={{0,8},{8,0},{1,9},{9,1},{2,10},{10,2},{3,11},{11,3},{4,12},{12,4},... | collective-permute-start | bytes 6291464 | tf_op jit(solution)/shard_map/ppermute | solution.py:71
  87.5 3.6 %collective-permute-start.4 = (bf16[64,8,1024]{2,1,0:T(8,128)(2,1)S(1)}, bf16[64,8,1024]{2,1,0:T(8,128)(2,1)S(1)}, u32[]{:S(2)}, u32[]{:S(2)}) collective-permute-start(bf16[64,8,1024]{2,1,0:T(8,128)(2,1)S(1)} %arrive_rest.1), channel_id=1, source_target_pairs={{0,8},{8,0},{1,9},{9,1},{2,10},{10,2},{3,11},{11,3},{4,12},{12,4},... | collective-permute-start | bytes 3145736 | tf_op jit(solution)/shard_map/ppermute | solution.py:71
  88.0 3.8 %collective-permute-start.3 = (bf16[64,8,1024]{2,1,0:T(8,128)(2,1)S(1)}, bf16[64,8,1024]{2,1,0:T(8,128)(2,1)S(1)}, u32[]{:S(2)}, u32[]{:S(2)}) collective-permute-start(bf16[64,8,1024]{2,1,0:T(8,128)(2,1)S(1)} %get-tuple-element.15), channel_id=1, source_target_pairs={{0,8},{8,0},{1,9},{9,1},{2,10},{10,2},{3,11},{11,3},{4,12},{12,4},... | collective-permute-start | bytes 3145736 | tf_op jit(solution)/shard_map/ppermute | solution.py:71
